TPU v7x, 32 devices: a whole 2x2x4 slice. The times are simulated.
32 devices in a mesh: gx: 4 (over y, core), gy: 8 (over z, x).
Axes of the slice: x: 2, y: 2, z: 4, core: 2. Of those that a mesh axis runs over, the one named last changes fastest.
Arguments:
- patches: bfloat16 [33856, 768], P(('gx', 'gy')), may hold values from -6 to 6
- cotangent: bfloat16 [33856, 768], P(('gx', 'gy')), may hold values from -6 to 6
- counts: int32 [64], P(('gx', 'gy')), may hold values from 40 to 529, as said below
- blank_mask: int32 [64, 529], P(('gx', 'gy')), may hold values 0 or 1
- ln1_gain: bfloat16 [768], P(('gx', 'gy')), may hold values from 0.25 to 1.75
- ln1_shift: bfloat16 [768], P(('gx', 'gy')), may hold values from -1.75 to 1.75
- w_qkv: bfloat16 [768, 2304], P(('gx', 'gy')), may hold values from -0.21875 to 0.21875
- query_bias: bfloat16 [768], P(('gx', 'gy')), may hold values from -3 to 3
- value_bias: bfloat16 [768], P(('gx', 'gy')), may hold values from -0.3125 to 0.3125
- w_proj: bfloat16 [768, 768], P(('gx', 'gy')), may hold values from -1.75 to 1.75
- proj_bias: bfloat16 [768], P(('gx', 'gy')), may hold values from -1.75 to 1.75
- ln2_gain: bfloat16 [768], P(('gx', 'gy')), may hold values from 0.25 to 1.75
- ln2_shift: bfloat16 [768], P(('gx', 'gy')), may hold values from -1.75 to 1.75
- w_up: bfloat16 [768, 3072], P(('gx', 'gy')), may hold values from -0.21875 to 0.21875
- up_bias: bfloat16 [3072], P(('gx', 'gy')), may hold values from -3 to 3
- w_down: bfloat16 [3072, 768], P(('gx', 'gy')), may hold values from -0.109375 to 0.109375
- down_bias: bfloat16 [768], P(('gx', 'gy')), may hold values from -1.75 to 1.75
Outputs:
- out_patches: bfloat16 [33856, 768], P(('gx', 'gy'))
- grad_patches: bfloat16 [33856, 768], P(('gx', 'gy'))
- grad_ln1_gain: float32 [768], P(('gx', 'gy'))
- grad_ln1_shift: float32 [768], P(('gx', 'gy'))
- grad_w_qkv: float32 [768, 2304], P(('gx', 'gy'))
- grad_query_bias: float32 [768], P(('gx', 'gy'))
- grad_value_bias: float32 [768], P(('gx', 'gy'))
- grad_w_proj: float32 [768, 768], P(('gx', 'gy'))
- grad_proj_bias: float32 [768], P(('gx', 'gy'))
- grad_ln2_gain: float32 [768], P(('gx', 'gy'))
- grad_ln2_shift: float32 [768], P(('gx', 'gy'))
- grad_w_up: float32 [768, 3072], P(('gx', 'gy'))
- grad_up_bias: float32 [3072], P(('gx', 'gy'))
- grad_w_down: float32 [3072, 768], P(('gx', 'gy'))
- grad_down_bias: float32 [768], P(('gx', 'gy'))
Inputs may be any that keep to these rules, and one draw needn't show every extreme that they name: `counts`: live patches of an item; one item has 529, another 529 // 13.
All inputs are finite; a program needn't handle non-finite values. No bound on the sum of `blank_mask` on one device may be relied on, other than what follows from the above.
Results may differ from a plain program's by a relative error of at most 0.013.
Values may be sent and summed in bfloat16 or wider, within the bound.
A program may use at most 192 MiB of HBM per device.

v0:
```python
from functools import partial

import jax
import jax.numpy as jnp
from jax import lax
from jax.sharding import PartitionSpec as P

HEAD_DIM = 64


epsilon = 1e-06


def normalize(matrix, scales, shifts):
    centre = jnp.mean(matrix, axis=-1, keepdims=True)
    centred = matrix - centre
    spread = jnp.mean(centred * centred, axis=-1, keepdims=True)
    return centred * lax.rsqrt(spread + epsilon) * scales + shifts


def split_heads(matrix):
    return matrix.reshape(matrix.shape[0], matrix.shape[1] // HEAD_DIM, HEAD_DIM)


def head_scores(queries, keys_all, allowed):
    raw = jnp.einsum(
        "qhd,khd->hqk",
        split_heads(queries),
        split_heads(keys_all),
        preferred_element_type=jnp.float32,
    )
    return jnp.where(allowed[None, None, :], raw * HEAD_DIM ** (-0.5), -1e30)


def attend_forward(pieces):
    queries, keys_all, values_all, allowed = pieces
    masked = head_scores(queries, keys_all, allowed)
    peak = jnp.max(masked, axis=-1, keepdims=True)
    log_total = peak + jnp.log(jnp.sum(jnp.exp(masked - peak), axis=-1, keepdims=True))
    probs = jnp.exp(masked - log_total)
    mixed_rows = jnp.einsum(
        "hqk,khd->qhd",
        probs.astype(jnp.bfloat16),
        split_heads(values_all),
        preferred_element_type=jnp.float32,
    )
    return (mixed_rows.reshape(queries.shape).astype(jnp.bfloat16), log_total)


def attend_backward(pieces):
    queries, keys_all, values_all, allowed, log_total, grad_mixed = pieces
    masked = head_scores(queries, keys_all, allowed)
    probs = jnp.exp(masked - log_total)
    grad_heads = split_heads(grad_mixed)
    grad_probs = jnp.einsum(
        "qhd,khd->hqk", grad_heads, split_heads(values_all), preferred_element_type=jnp.float32
    )
    inner = jnp.sum(grad_probs * probs, axis=-1, keepdims=True)
    grad_scores = (probs * (grad_probs - inner)).astype(jnp.bfloat16)
    scale_factor = HEAD_DIM ** (-0.5)
    grad_query = (
        jnp.einsum(
            "hqk,khd->qhd", grad_scores, split_heads(keys_all), preferred_element_type=jnp.float32
        )
        * scale_factor
    )
    grad_key = (
        jnp.einsum(
            "hqk,qhd->khd", grad_scores, split_heads(queries), preferred_element_type=jnp.float32
        )
        * scale_factor
    )
    grad_value = jnp.einsum(
        "hqk,qhd->khd", probs.astype(jnp.bfloat16), grad_heads, preferred_element_type=jnp.float32
    )
    joined = jnp.concatenate(
        [
            grad_query.reshape(queries.shape),
            grad_key.reshape(queries.shape),
            grad_value.reshape(queries.shape),
        ],
        axis=-1,
    )
    return joined.astype(jnp.bfloat16)


def local(
    patches,
    cotangent,
    counts,
    blank_mask,
    ln1_gain,
    ln1_shift,
    w_qkv,
    query_bias,
    value_bias,
    w_proj,
    proj_bias,
    ln2_gain,
    ln2_shift,
    w_up,
    up_bias,
    w_down,
    down_bias,
):
    items_here = counts.shape[0]
    length = blank_mask.shape[1]
    width = patches.shape[1]
    positions = jnp.arange(length, dtype=jnp.int32)
    live_mask = positions[None, :] < counts[:, None]
    allowed = live_mask & ((blank_mask == 1) | (positions[None, :] == 0))
    live_rows = live_mask.reshape(-1, 1).astype(jnp.float32)
    attn_full = (
        lax.all_gather(ln1_gain, ("gx", "gy"), axis=0, tiled=True),
        lax.all_gather(ln1_shift, ("gx", "gy"), axis=0, tiled=True),
        lax.all_gather(w_qkv, ("gx", "gy"), axis=0, tiled=True),
        lax.all_gather(query_bias, ("gx", "gy"), axis=0, tiled=True),
        lax.all_gather(value_bias, ("gx", "gy"), axis=0, tiled=True),
        lax.all_gather(w_proj, ("gx", "gy"), axis=0, tiled=True),
        lax.all_gather(proj_bias, ("gx", "gy"), axis=0, tiled=True),
    )
    gain_one, shift_one, qkv_weight, bias_query, bias_value, proj_weight, bias_proj = attn_full
    inputs = patches.astype(jnp.float32)
    gain_float = gain_one.astype(jnp.float32)
    shift_float = shift_one.astype(jnp.float32)
    normed_low = normalize(inputs, gain_float, shift_float).astype(jnp.bfloat16)
    projected = jnp.dot(normed_low, qkv_weight, preferred_element_type=jnp.float32)
    queries = (projected[:, :width] + bias_query.astype(jnp.float32)).astype(jnp.bfloat16)
    keys_all = projected[:, width : 2 * width].astype(jnp.bfloat16)
    values_all = (projected[:, 2 * width :] + bias_value.astype(jnp.float32)).astype(jnp.bfloat16)
    per_item = (
        queries.reshape(items_here, length, width),
        keys_all.reshape(items_here, length, width),
        values_all.reshape(items_here, length, width),
        allowed,
    )
    mixed_items, log_totals = lax.map(attend_forward, per_item)
    mixed_low = mixed_items.reshape(-1, width)
    residual = (
        inputs
        + jnp.dot(mixed_low, proj_weight, preferred_element_type=jnp.float32)
        + bias_proj.astype(jnp.float32)
    )
    mlp_full = (
        lax.all_gather(ln2_gain, ("gx", "gy"), axis=0, tiled=True),
        lax.all_gather(ln2_shift, ("gx", "gy"), axis=0, tiled=True),
        lax.all_gather(w_up, ("gx", "gy"), axis=0, tiled=True),
        lax.all_gather(up_bias, ("gx", "gy"), axis=0, tiled=True),
        lax.all_gather(w_down, ("gx", "gy"), axis=0, tiled=True),
        lax.all_gather(down_bias, ("gx", "gy"), axis=0, tiled=True),
    )
    gain_two, shift_two, up_weight, bias_up, down_weight, bias_down = mlp_full
    normed_two = normalize(
        residual, gain_two.astype(jnp.float32), shift_two.astype(jnp.float32)
    ).astype(jnp.bfloat16)
    pre_act = jnp.dot(normed_two, up_weight, preferred_element_type=jnp.float32) + bias_up.astype(
        jnp.float32
    )
    activated, gelu_back = jax.vjp(partial(jax.nn.gelu, approximate=False), pre_act)
    act_low = activated.astype(jnp.bfloat16)
    out_branch = jnp.dot(
        act_low, down_weight, preferred_element_type=jnp.float32
    ) + bias_down.astype(jnp.float32)
    output = ((residual + out_branch) * live_rows).astype(jnp.bfloat16)
    mlp_back = (
        lax.all_gather(ln2_gain, ("gx", "gy"), axis=0, tiled=True),
        lax.all_gather(ln2_shift, ("gx", "gy"), axis=0, tiled=True),
        lax.all_gather(w_up, ("gx", "gy"), axis=0, tiled=True),
        lax.all_gather(up_bias, ("gx", "gy"), axis=0, tiled=True),
        lax.all_gather(w_down, ("gx", "gy"), axis=0, tiled=True),
        lax.all_gather(down_bias, ("gx", "gy"), axis=0, tiled=True),
    )
    gain_two_b, shift_two_b, up_weight_b, bias_up_b, down_weight_b, bias_down_b = mlp_back
    grad_out = cotangent.astype(jnp.float32) * live_rows
    grad_down_low = grad_out.astype(jnp.bfloat16)
    down_grad = jnp.einsum("tf,td->fd", act_low, grad_down_low, preferred_element_type=jnp.float32)
    down_bias_grad = jnp.sum(grad_down_low.astype(jnp.float32), axis=0)
    grad_act = jnp.einsum(
        "td,fd->tf", grad_down_low, down_weight_b, preferred_element_type=jnp.float32
    )
    grad_pre_low = gelu_back(grad_act)[0].astype(jnp.bfloat16)
    up_grad = jnp.einsum("td,tf->df", normed_two, grad_pre_low, preferred_element_type=jnp.float32)
    up_bias_grad = jnp.sum(grad_pre_low.astype(jnp.float32), axis=0)
    grad_normed_two = jnp.einsum(
        "tf,df->td", grad_pre_low, up_weight_b, preferred_element_type=jnp.float32
    )
    _, norm_back_two = jax.vjp(
        normalize, residual, gain_two_b.astype(jnp.float32), shift_two_b.astype(jnp.float32)
    )
    grad_resid_part, gain_two_grad, shift_two_grad = norm_back_two(grad_normed_two)
    grad_resid = grad_out + grad_resid_part
    mlp_owned = (
        lax.psum_scatter(gain_two_grad, ("gx", "gy"), scatter_dimension=0, tiled=True),
        lax.psum_scatter(shift_two_grad, ("gx", "gy"), scatter_dimension=0, tiled=True),
        lax.psum_scatter(up_grad, ("gx", "gy"), scatter_dimension=0, tiled=True),
        lax.psum_scatter(up_bias_grad, ("gx", "gy"), scatter_dimension=0, tiled=True),
        lax.psum_scatter(down_grad, ("gx", "gy"), scatter_dimension=0, tiled=True),
        lax.psum_scatter(down_bias_grad, ("gx", "gy"), scatter_dimension=0, tiled=True),
    )
    attn_back = (
        lax.all_gather(ln1_gain, ("gx", "gy"), axis=0, tiled=True),
        lax.all_gather(ln1_shift, ("gx", "gy"), axis=0, tiled=True),
        lax.all_gather(w_qkv, ("gx", "gy"), axis=0, tiled=True),
        lax.all_gather(query_bias, ("gx", "gy"), axis=0, tiled=True),
        lax.all_gather(value_bias, ("gx", "gy"), axis=0, tiled=True),
        lax.all_gather(w_proj, ("gx", "gy"), axis=0, tiled=True),
        lax.all_gather(proj_bias, ("gx", "gy"), axis=0, tiled=True),
    )
    (
        gain_one_b,
        shift_one_b,
        qkv_weight_b,
        bias_query_b,
        bias_value_b,
        proj_weight_b,
        bias_proj_b,
    ) = attn_back
    grad_branch_low = grad_resid.astype(jnp.bfloat16)
    proj_grad = jnp.einsum(
        "td,te->de", mixed_low, grad_branch_low, preferred_element_type=jnp.float32
    )
    proj_bias_grad = jnp.sum(grad_branch_low.astype(jnp.float32), axis=0)
    grad_mixed = jnp.einsum(
        "te,de->td", grad_branch_low, proj_weight_b, preferred_element_type=jnp.float32
    ).astype(jnp.bfloat16)
    back_items = (
        per_item[0],
        per_item[1],
        per_item[2],
        allowed,
        log_totals,
        grad_mixed.reshape(items_here, length, width),
    )
    grad_projected = lax.map(attend_backward, back_items).reshape(-1, 3 * width)
    qkv_grad = jnp.einsum(
        "td,te->de", normed_low, grad_projected, preferred_element_type=jnp.float32
    )
    query_bias_grad = jnp.sum(grad_projected[:, :width].astype(jnp.float32), axis=0)
    value_bias_grad = jnp.sum(grad_projected[:, 2 * width :].astype(jnp.float32), axis=0)
    grad_normed = jnp.einsum(
        "te,de->td", grad_projected, qkv_weight_b, preferred_element_type=jnp.float32
    )
    _, norm_back_one = jax.vjp(
        normalize, inputs, gain_one_b.astype(jnp.float32), shift_one_b.astype(jnp.float32)
    )
    grad_input_part, gain_one_grad, shift_one_grad = norm_back_one(grad_normed)
    grad_input = (grad_resid + grad_input_part).astype(jnp.bfloat16)
    attn_owned = (
        lax.psum_scatter(gain_one_grad, ("gx", "gy"), scatter_dimension=0, tiled=True),
        lax.psum_scatter(shift_one_grad, ("gx", "gy"), scatter_dimension=0, tiled=True),
        lax.psum_scatter(qkv_grad, ("gx", "gy"), scatter_dimension=0, tiled=True),
        lax.psum_scatter(query_bias_grad, ("gx", "gy"), scatter_dimension=0, tiled=True),
        lax.psum_scatter(value_bias_grad, ("gx", "gy"), scatter_dimension=0, tiled=True),
        lax.psum_scatter(proj_grad, ("gx", "gy"), scatter_dimension=0, tiled=True),
        lax.psum_scatter(proj_bias_grad, ("gx", "gy"), scatter_dimension=0, tiled=True),
    )
    owned_all = attn_owned + mlp_owned
    return (
        output,
        grad_input,
        owned_all[0],
        owned_all[1],
        owned_all[2],
        owned_all[3],
        owned_all[4],
        owned_all[5],
        owned_all[6],
        owned_all[7],
        owned_all[8],
        owned_all[9],
        owned_all[10],
        owned_all[11],
        owned_all[12],
    )


def solution(mesh):
    placed = (
        P(("gx", "gy"), None),
        P(("gx", "gy"), None),
        P(("gx", "gy")),
        P(("gx", "gy"), None),
        P(("gx", "gy")),
        P(("gx", "gy")),
        P(("gx", "gy"), None),
        P(("gx", "gy")),
        P(("gx", "gy")),
        P(("gx", "gy"), None),
        P(("gx", "gy")),
        P(("gx", "gy")),
        P(("gx", "gy")),
        P(("gx", "gy"), None),
        P(("gx", "gy")),
        P(("gx", "gy"), None),
        P(("gx", "gy")),
    )
    return jax.shard_map(
        local,
        mesh=mesh,
        in_specs=placed,
        out_specs=(
            P(("gx", "gy"), None),
            P(("gx", "gy"), None),
            P(("gx", "gy")),
            P(("gx", "gy")),
            P(("gx", "gy"), None),
            P(("gx", "gy")),
            P(("gx", "gy")),
            P(("gx", "gy"), None),
            P(("gx", "gy")),
            P(("gx", "gy")),
            P(("gx", "gy")),
            P(("gx", "gy"), None),
            P(("gx", "gy")),
            P(("gx", "gy"), None),
            P(("gx", "gy")),
        ),
        check_vma=False,
    )
```

profile of v0, /device:TPU:0, one launch (start us, length us, event | category | flops | bytes accessed | tf_op | source)
XLA Modules:
  0.0 835.8 jit_solution(4755801841289871624)
XLA Ops:
  17.6 42.7 %all-reduce.19 = (bf16[768]{0:T(1024)(128)(2,1)S(1)}, bf16[768]{0:T(1024)(128)(2,1)S(1)}, bf16[768]{0:T(1024)(128)(2,1)S(1)}, bf16[768]{0:T(1024)(128)(2,1)S(1)}...) all-reduce(bf16[768]{0:T(1024)(128)(2,1)S(1)} %dynamic-update-slice, ...), channel_id=1, replica_groups=mesh['gx'=4,'gy'=8] {'gx','gy'}, use_global_device_ids=true, to_apply=%add.1 | all-reduce | flops 9216 | bytes 36864
  64.3 9.9 %all-gather.5.cloned.1.call-done = bf16[768,2304]{1,0:T(8,128)(2,1)} async-done(((bf16[24,2304]{1,0:T(8,128)(2,1)}), bf16[768,2304]{1,0:T(8,128)(2,1)}) %all-gather.5.cloned.1.call-update) | async-done | bytes 3538960 | tf_op jit(solution)/shard_map/all_gather | solution.py:116
  74.2 6.4 fusion.44
  85.5 2.7 copy.62
  88.3 3.9 copy.61
  92.1 2.9 reshape.265
  95.0 3.9 copy.60
  98.9 66.1 %while.22 = (s32[]{:T(128)}, bf16[2,529,768]{2,1,0:T(8,128)(2,1)}, f32[2,12,529,1]{2,1,3,0:T(8,128)S(1)}, bf16[2,529,768]{1,2,0:T(8,128)(2,1)}, pred[2,529]{1,0:...) while((s32[]{:T(128)}, bf16[2,529,768]{2,1,0:T(8,128)(2,1)}, ...), condition=%wide.region_5.6_spmd, body=%wide.region_2.5_spmd.sunk | while | flops 897010432 | bytes 51951636 | solution.py:137
  101.9 7.6 fusion.103
  109.5 9.2 %exponential_reduce_fusion.2 = f32[12,529]{1,0:T(8,128)S(1)} fusion(f32[12,529,529]{1,2,0:T(8,128)} %get-tuple-element.324, f32[12,529]{1,0:T(8,128)S(1)} %get-tuple-element.325, pred[529]{0:T(1024)(128)(4,1)S(1)} %dynamic-slice_reduce_fusion.4), kind=kLoop, calls=%fused_computation.1.clone.1 | loop fusion | flops 13426020 | bytes 13483681 | tf_op jit(solution)/shard_map/while/body/eval_jaxpr/reduce_sum | solution.py:39
  118.7 10.6 %fusion.104 = bf16[12,64,529]{2,1,0:T(8,128)(2,1)} fusion(bf16[529,12,64]{0,2,1:T(8,128)(2,1)S(1)} %bitcast.116, f32[12,529,529]{1,2,0:T(8,128)} %get-tuple-element.324, f32[12,529]{1,0:T(8,128)S(1)} %get-tuple-element.326, pred[529]{0:T(1024)(128)(4,1)S(1)} %dynamic-slice_reduce_fusion.4), kind=kOutput, calls=%fused_computation.6.clone.1 | convolution fusion | flops 443674432 | bytes 15083377 | tf_op jit(solution)/shard_map/while/body/eval_jaxpr/hqk,khd->qhd/dot_general | solution.py:41
  134.6 7.8 fusion.103
  142.3 9.2 %exponential_reduce_fusion.2 = f32[12,529]{1,0:T(8,128)S(1)} fusion(f32[12,529,529]{1,2,0:T(8,128)} %get-tuple-element.324, f32[12,529]{1,0:T(8,128)S(1)} %get-tuple-element.325, pred[529]{0:T(1024)(128)(4,1)S(1)} %dynamic-slice_reduce_fusion.4), kind=kLoop, calls=%fused_computation.1.clone.1 | loop fusion | flops 13426020 | bytes 13483681 | tf_op jit(solution)/shard_map/while/body/eval_jaxpr/reduce_sum | solution.py:39
  151.6 10.5 %fusion.104 = bf16[12,64,529]{2,1,0:T(8,128)(2,1)} fusion(bf16[529,12,64]{0,2,1:T(8,128)(2,1)S(1)} %bitcast.116, f32[12,529,529]{1,2,0:T(8,128)} %get-tuple-element.324, f32[12,529]{1,0:T(8,128)S(1)} %get-tuple-element.326, pred[529]{0:T(1024)(128)(4,1)S(1)} %dynamic-slice_reduce_fusion.4), kind=kOutput, calls=%fused_computation.6.clone.1 | convolution fusion | flops 443674432 | bytes 15083377 | tf_op jit(solution)/shard_map/while/body/eval_jaxpr/hqk,khd->qhd/dot_general | solution.py:41
  165.0 3.6 reshape.268
  168.7 3.9 fusion.52
  174.9 21.1 %all-gather.9.cloned.1.call-done = bf16[768,3072]{1,0:T(8,128)(2,1)} async-done(((bf16[24,3072]{1,0:T(8,128)(2,1)}), bf16[768,3072]{1,0:T(8,128)(2,1)}) %all-gather.9.cloned.1.call-update) | async-done | bytes 4718608 | tf_op jit(solution)/shard_map/all_gather | solution.py:147
  196.0 38.2 %multiply_convert_fusion.3 = (bf16[1058,3072]{1,0:T(8,128)(2,1)}, f32[1058,3072]{1,0:T(8,128)}, f32[1058,3072]{1,0:T(8,128)}) fusion(f32[3072]{0:T(1024)S(1)} %convert_element_type.140, bf16[768,3072]{1,0:T(8,128)(2,1)} %all-gather.9.cloned.1.call-done, f32[1058,768]{1,0:T(8,128)} %copy-done.1, f32[768]{0:T(1024)S(1)} %convert_element_type.138, ...), kind=kOutput, calls=%fused_computation.37 | convolution fusion | flops 5210844672 | bytes 40497424 | tf_op jit(solution)/shard_map/dot_general | solution.py:156
  234.2 27.2 %all-gather.11.cloned.1.call-done = bf16[3072,768]{1,0:T(8,128)(2,1)} async-done(((bf16[96,768]{1,0:T(8,128)(2,1)}), bf16[3072,768]{1,0:T(8,128)(2,1)}) %all-gather.11.cloned.1.call-update) | async-done | bytes 4718608 | tf_op jit(solution)/shard_map/all_gather | solution.py:149
  261.4 17.9 %convert_reduce_fusion = (f32[3072]{0:T(1024)}, bf16[1058,3072]{1,0:T(8,128)(2,1)}) fusion(f32[1058,3072]{1,0:T(8,128)} %get-tuple-element.207, f32[1058,3072]{1,0:T(8,128)} %get-tuple-element.223, bf16[3072,768]{1,0:T(8,128)(2,1)} %all-gather.11.cloned.1.call-done, bf16[1058,768]{1,0:T(8,128)(2,1)} %param.22, f32[1058]{0:T(1024)S(1)} %copy-done.28), kind=kOutput, calls=%fused_computation.35 | convolution fusion | flops 5046707712 | bytes 38861960 | tf_op jit(solution)/shard_map/td,fd->tf/dot_general | solution.py:178
  279.3 10.7 %multiply_reduce_fusion.1 = (f32[768]{0:T(1024)}, f32[1058]{0:T(1024)S(1)}, f32[768]{0:T(1024)}, f32[1058,768]{1,0:T(8,128)S(1)}) fusion(f32[1058,768]{1,0:T(8,128)S(1)} %copy-done.2, f32[1058]{0:T(1024)S(1)} %fusion.37, f32[1058]{0:T(1024)S(1)} %broadcast_multiply_fusion, f32[768]{0:T(1024)S(1)} %convert_element_type.137, ...), kind=kOutput, calls=%fused_computation.79 | convolution fusion | flops 4998767616 | bytes 17741208 | tf_op jit(solution)/shard_map/tf,df->td/dot_general | solution.py:184
  293.8 3.2 fusion.53
  301.5 109.7 %while.23 = (s32[]{:T(128)}, bf16[2,529,2304]{2,1,0:T(8,128)(2,1)}, bf16[2,529,768]{1,2,0:T(8,128)(2,1)}, pred[2,529]{1,0:T(4,128)(4,1)S(1)}, bf16[2,529,768]{1,...) while((s32[]{:T(128)}, bf16[2,529,2304]{2,1,0:T(8,128)(2,1)}, ...), condition=%wide.region_12.13_spmd, body=%wide.region_10.12_spmd.sunk | while | flops 2188739584 | bytes 144813360 | solution.py:234
  306.5 8.0 subtract_exponential_fusion.2
  314.5 8.6 %fusion.115 = bf16[12,64,529]{2,1,0:T(8,128)(2,1)S(1)} fusion(bf16[529,12,64]{0,2,1:T(8,128)(2,1)S(1)} %bitcast.103, f32[12,529,529]{1,2,0:T(8,128)} %subtract_exponential_fusion.2), kind=kOutput, calls=%fused_computation.24.clone.1 | convolution fusion | flops 433600128 | bytes 15057456 | tf_op jit(solution)/shard_map/while/body/eval_jaxpr/hqk,qhd->khd/dot_general | solution.py:73
  323.1 10.8 %multiply_reduce_fusion.5 = (f32[12,529]{1,0:T(8,128)S(1)}, f32[12,529,529]{1,2,0:T(8,128)}) fusion(f32[12,529,529]{1,2,0:T(8,128)} %subtract_exponential_fusion.2, bf16[529,12,64]{0,2,1:T(8,128)(2,1)S(1)} %bitcast.104, bf16[529,12,64]{0,2,1:T(8,128)(2,1)S(1)} %bitcast.111), kind=kOutput, calls=%fused_computation.17.clone.1 | convolution fusion | flops 436545600 | bytes 28515216 | tf_op jit(solution)/shard_map/while/body/eval_jaxpr/qhd,khd->hqk/dot_general | solution.py:55
  333.9 11.3 %multiply_convert_fusion.7 = bf16[12,529,529]{1,2,0:T(8,128)(2,1)S(1)} fusion(f32[12,529,529]{1,2,0:T(8,128)} %subtract_exponential_fusion.2, f32[12,529,529]{1,2,0:T(8,128)} %get-tuple-element.338, f32[12,529]{1,0:T(8,128)S(1)} %get-tuple-element.339), kind=kLoop, calls=%fused_computation.16.clone.1 | loop fusion | flops 10074276 | bytes 33606312 | tf_op jit(solution)/shard_map/while/body/eval_jaxpr/convert_element_type | solution.py:59
  346.9 2.7 multiply_convert_fusion.8
  349.9 3.4 copy.83
  353.3 3.5 constant_dynamic-update-slice_fusion.5
  361.4 7.9 subtract_exponential_fusion.2
  369.3 8.5 %fusion.115 = bf16[12,64,529]{2,1,0:T(8,128)(2,1)S(1)} fusion(bf16[529,12,64]{0,2,1:T(8,128)(2,1)S(1)} %bitcast.103, f32[12,529,529]{1,2,0:T(8,128)} %subtract_exponential_fusion.2), kind=kOutput, calls=%fused_computation.24.clone.1 | convolution fusion | flops 433600128 | bytes 15057456 | tf_op jit(solution)/shard_map/while/body/eval_jaxpr/hqk,qhd->khd/dot_general | solution.py:73
  377.8 10.6 %multiply_reduce_fusion.5 = (f32[12,529]{1,0:T(8,128)S(1)}, f32[12,529,529]{1,2,0:T(8,128)}) fusion(f32[12,529,529]{1,2,0:T(8,128)} %subtract_exponential_fusion.2, bf16[529,12,64]{0,2,1:T(8,128)(2,1)S(1)} %bitcast.104, bf16[529,12,64]{0,2,1:T(8,128)(2,1)S(1)} %bitcast.111), kind=kOutput, calls=%fused_computation.17.clone.1 | convolution fusion | flops 436545600 | bytes 28515216 | tf_op jit(solution)/shard_map/while/body/eval_jaxpr/qhd,khd->hqk/dot_general | solution.py:55
  388.3 11.3 %multiply_convert_fusion.7 = bf16[12,529,529]{1,2,0:T(8,128)(2,1)S(1)} fusion(f32[12,529,529]{1,2,0:T(8,128)} %subtract_exponential_fusion.2, f32[12,529,529]{1,2,0:T(8,128)} %get-tuple-element.338, f32[12,529]{1,0:T(8,128)S(1)} %get-tuple-element.339), kind=kLoop, calls=%fused_computation.16.clone.1 | loop fusion | flops 10074276 | bytes 33606312 | tf_op jit(solution)/shard_map/while/body/eval_jaxpr/convert_element_type | solution.py:59
  404.3 3.4 copy.83
  407.7 3.5 constant_dynamic-update-slice_fusion.5
  411.2 5.8 reshape.270
  417.0 9.8 %fusion.42 = f32[768,2304]{1,0:T(8,128)} fusion(bf16[1058,2304]{1,0:T(8,128)(2,1)} %reshape.270, bf16[1058,768]{1,0:T(8,128)(2,1)S(1)} %copy-done.6, f32[768]{0:T(1024)S(1)} %copy-done.40, f32[768]{0:T(1024)S(1)} %copy-done.35, f32[1058]{0:T(1024)S(1)} %copy-done.25, f32[1058]{0:T(1024)S(1)} %copy-done.21), kind=kOutput, calls=%fused_computation.106 | convolution fusion | flops 3749078016 | bytes 13592848 | tf_op jit(solution)/shard_map/td,te->de/dot_general | solution.py:235
  428.7 12.1 %fusion.47 = f32[768,3072]{1,0:T(8,128)} fusion(bf16[1058,3072]{1,0:T(8,128)(2,1)} %get-tuple-element.227, f32[1058,768]{1,0:T(8,128)S(1)} %copy-done.3, f32[768]{0:T(1024)S(1)} %copy-done.33, f32[768]{0:T(1024)S(1)} %copy-done.23, f32[1058]{0:T(1024)S(1)} %copy-done.19, f32[1058]{0:T(1024)S(1)} %copy-done.17), kind=kOutput, calls=%fused_computation.109 | convolution fusion | flops 4996333056 | bytes 19202320 | tf_op jit(solution)/shard_map/td,tf->df/dot_general | solution.py:182
  441.5 11.7 %fusion.39 = f32[3072,768]{1,0:T(8,128)} fusion(bf16[1058,3072]{1,0:T(8,128)(2,1)} %get-tuple-element.206, bf16[1058,768]{1,0:T(8,128)(2,1)} %param.22, f32[1058]{0:T(1024)S(1)} %copy-done.29), kind=kOutput, calls=%fused_computation.105 | convolution fusion | flops 4994707968 | bytes 17566856 | tf_op jit(solution)/shard_map/tf,td->fd/dot_general | solution.py:176
  453.9 8.7 %fusion.48 = (f32[768]{0:T(1024)S(1)}, f32[1058]{0:T(1024)S(1)}, f32[1058,768]{1,0:T(8,128)S(1)}) fusion(f32[768]{0:T(1024)S(1)} %copy-done.35, f32[1058]{0:T(1024)S(1)} %copy-done.21, bf16[1058,768]{1,0:T(8,128)(2,1)} %param.21, bf16[1058,2304]{1,0:T(8,128)(2,1)} %reshape.270, bf16[768,2304]{1,0:T(8,128)(2,1)} %all-gather.5.cloned.1.call-done), kind=kOutput, calls=%fused_computation.110 | convolution fusion | flops 3749076224 | bytes 13304080 | tf_op jit(solution)/shard_map/te,de->td/dot_general | solution.py:240
  462.6 3.8 convert_reduce_fusion.4
  468.2 42.5 %all-reduce.18 = (f32[768]{0:T(1024)S(1)}, f32[768]{0:T(1024)S(1)}, f32[768]{0:T(1024)S(1)}, f32[768]{0:T(1024)S(1)}, f32[768]{0:T(1024)S(1)}, /*index=5*/f32[76...) all-reduce(f32[768]{0:T(1024)S(1)} %get-tuple-element.145, ...), channel_id=2, replica_groups=mesh['gx'=4,'gy'=8] {'gx','gy'}, use_global_device_ids=true, to_apply=%region_16.17.clone | all-reduce | flops 9216 | bytes 73728
  515.9 5.6 add_convert_fusion.1
  521.5 9.8 %fusion.26 = bf16[1058,768]{1,0:T(8,128)(2,1)} fusion(f32[1058,768]{1,0:T(8,128)S(1)} %copy-done.3, bf16[1058,3072]{1,0:T(8,128)(2,1)} %get-tuple-element.206, bf16[3072,768]{1,0:T(8,128)(2,1)} %all-gather.11.cloned.1.call-done, f32[1058]{0:T(1024)S(1)} %copy-done.29, f32[768]{0:T(1024)S(1)} %convert_element_type.142), kind=kOutput, calls=%fused_computation.67 | convolution fusion | flops 4995520512 | bytes 16101512 | tf_op jit(solution)/shard_map/dot_general | solution.py:161
  531.3 13.9 %reduce-scatter.5.cloned.1.call-done = f32[24,2304]{1,0:T(8,128)} async-done(((f32[768,2304]{1,0:T(8,128)}), f32[24,2304]{1,0:T(8,128)}) %reduce-scatter.5.cloned.1.call-update) | async-done | bytes 221200 | tf_op jit(solution)/shard_map/reduce_scatter | solution.py:251
  545.2 141.5 %reduce-scatter.9.cloned.1.call-done = f32[24,3072]{1,0:T(8,128)} async-done(((f32[768,3072]{1,0:T(8,128)}), f32[24,3072]{1,0:T(8,128)}) %reduce-scatter.9.cloned.1.call-update) | async-done | bytes 294928 | tf_op jit(solution)/shard_map/reduce_scatter | solution.py:195
  686.7 142.0 %reduce-scatter.11.cloned.1.call-done = f32[96,768]{1,0:T(8,128)} async-done(((f32[3072,768]{1,0:T(8,128)}), f32[96,768]{1,0:T(8,128)}) %reduce-scatter.11.cloned.1.call-update) | async-done | bytes 294928 | tf_op jit(solution)/shard_map/reduce_scatter | solution.py:197
  (203 shorter events, 66.3 us)
Async XLA Ops:
  7.2 56.4 %copy-start.5 = (bf16[1058,768]{1,0:T(8,128)(2,1)S(1)}, bf16[1058,768]{1,0:T(8,128)(2,1)}, u32[]{:S(2)}) copy-start(bf16[1058,768]{1,0:T(8,128)(2,1)} %param.21) | copy-start | bytes 4875268
  7.2 67.0 %all-gather.5.cloned.1.call-start = ((), (), s32[]{:S(2)}) async-start(), calls=%async_computation.4 | async-start | bytes 3649536 | tf_op jit(solution)/shard_map/all_gather | solution.py:116
  7.9 160.7 %all-gather.7.cloned.1.call-start = ((), (), s32[]{:S(2)}) async-start(), calls=%async_computation.5 | async-start | bytes 1216512 | tf_op jit(solution)/shard_map/all_gather | solution.py:119
  8.7 187.3 %all-gather.9.cloned.1.call-start = ((), (), s32[]{:S(2)}) async-start(), calls=%async_computation.6 | async-start | bytes 4866048 | tf_op jit(solution)/shard_map/all_gather | solution.py:147
  9.4 251.9 %all-gather.11.cloned.1.call-start = ((), (), s32[]{:S(2)}) async-start(), calls=%async_computation.7 | async-start | bytes 4866048 | tf_op jit(solution)/shard_map/all_gather | solution.py:149
  10.0 521.3 %reduce-scatter.7.cloned.1.call-start = ((), (), s32[]{:S(2)}) async-start(), calls=%async_computation.9 | async-start | bytes 2433024 | tf_op jit(solution)/shard_map/reduce_scatter | solution.py:254
  60.3 20.2 %copy-start.39 = (f32[768]{0:T(1024)}, f32[768]{0:T(1024)S(1)}, u32[]{:S(2)}) copy-start(f32[768]{0:T(1024)S(1)} %convert_element_type.130) | copy-start | bytes 9220
  60.3 20.2 %copy-start.34 = (f32[768]{0:T(1024)}, f32[768]{0:T(1024)S(1)}, u32[]{:S(2)}) copy-start(f32[768]{0:T(1024)S(1)} %convert_element_type.129) | copy-start | bytes 9220
  60.4 229.6 %copy-start.22 = (f32[768]{0:T(1024)}, f32[768]{0:T(1024)S(1)}, u32[]{:S(2)}) copy-start(f32[768]{0:T(1024)S(1)} %convert_element_type.137) | copy-start | bytes 9220
  60.4 135.6 %copy-start.32 = (f32[768]{0:T(1024)}, f32[768]{0:T(1024)S(1)}, u32[]{:S(2)}) copy-start(f32[768]{0:T(1024)S(1)} %convert_element_type.138) | copy-start | bytes 9220
  63.6 16.9 %copy-start.20 = (f32[1058]{0:T(1024)}, f32[1058]{0:T(1024)S(1)}, u32[]{:S(2)}) copy-start(f32[1058]{0:T(1024)S(1)} %broadcast_multiply_fusion.1) | copy-start | bytes 12700
  64.3 16.3 %copy-start.30 = (f32[1058]{0:T(1024)}, f32[1058]{0:T(1024)S(1)}, u32[]{:S(2)}) copy-start(f32[1058]{0:T(1024)S(1)} %fusion.30) | copy-start | bytes 12700
  64.3 16.3 %copy-start.24 = (f32[1058]{0:T(1024)}, f32[1058]{0:T(1024)S(1)}, u32[]{:S(2)}) copy-start(f32[1058]{0:T(1024)S(1)} %fusion.36) | copy-start | bytes 12700
  165.0 7.6 copy-start
  165.0 7.6 copy-start.13
  165.0 7.6 copy-start.14
  172.6 1.7 copy-start.1
  172.6 117.4 %copy-start.16 = (f32[1058]{0:T(1024)}, f32[1058]{0:T(1024)S(1)}, u32[]{:S(2)}) copy-start(f32[1058]{0:T(1024)S(1)} %broadcast_multiply_fusion) | copy-start | bytes 12700
  174.9 115.1 %copy-start.18 = (f32[1058]{0:T(1024)}, f32[1058]{0:T(1024)S(1)}, u32[]{:S(2)}) copy-start(f32[1058]{0:T(1024)S(1)} %fusion.37) | copy-start | bytes 12700
  174.9 86.4 %copy-start.28 = (f32[1058]{0:T(1024)S(1)}, f32[1058]{0:T(1024)}, u32[]{:S(2)}) copy-start(f32[1058]{0:T(1024)} %reshape.271) | copy-start | bytes 12700
  261.3 17.9 %copy-start.2 = (f32[1058,768]{1,0:T(8,128)S(1)}, f32[1058,768]{1,0:T(8,128)}, u32[]{:S(2)}) copy-start(f32[1058,768]{1,0:T(8,128)} %copy-done.1) | copy-start | bytes 9750532
  291.5 2.4 copy-start.12
  293.8 3.2 copy-start.44
  297.0 248.2 %reduce-scatter.5.cloned.1.call-start = ((), (), s32[]{:S(2)}) async-start(), calls=%async_computation.8 | async-start | bytes 7299072 | tf_op jit(solution)/shard_map/reduce_scatter | solution.py:251
  299.7 1.8 copy-start.15
  301.9 4.6 copy-start.8
  353.3 3.5 copy-start.9
  356.8 4.5 copy-start.8
  407.7 3.5 copy-start.9
  411.2 5.8 copy-start.6
  411.2 5.8 copy-start.21
  411.2 5.8 copy-start.25
  411.2 5.8 copy-start.35
  411.2 5.8 copy-start.40
  426.8 1.9 copy-start.3
  426.8 1.9 copy-start.17
  426.8 1.9 copy-start.19
  426.8 1.9 copy-start.23
  426.8 1.9 copy-start.33
  426.8 259.9 %reduce-scatter.9.cloned.1.call-start = ((), (), s32[]{:S(2)}) async-start(), calls=%async_computation.10 | async-start | bytes 9732096 | tf_op jit(solution)/shard_map/reduce_scatter | solution.py:195
  440.8 387.9 %reduce-scatter.11.cloned.1.call-start = ((), (), s32[]{:S(2)}) async-start(), calls=%async_computation.11 | async-start | bytes 9732096 | tf_op jit(solution)/shard_map/reduce_scatter | solution.py:197
  453.9 8.7 %copy-start.31 = (f32[1058]{0:T(1024)S(1)}, f32[1058]{0:T(1024)}, u32[]{:S(2)}) copy-start(f32[1058]{0:T(1024)} %copy-done.30) | copy-start | bytes 12700
  462.5 5.6 copy-start.10
  462.6 3.9 copy-start.7
  466.4 1.7 copy-start.36
  466.4 1.7 copy-start.37
  466.4 1.7 copy-start.38
  466.4 49.5 %copy-start.27 = (f32[1058]{0:T(1024)S(1)}, f32[1058]{0:T(1024)}, u32[]{:S(2)}) copy-start(f32[1058]{0:T(1024)} %copy-done.26) | copy-start | bytes 12700
  (7 other events, 9.6 us)
Sparse Core Ops, SparseCore 0:
  11.0 63.1 all-gather.4
  77.2 53.1 all-gather.6
  133.3 62.6 all-gather.8
  198.8 62.4 all-gather.10
  297.1 97.8 reduce-scatter.6
  427.0 118.2 reduce-scatter.4
  551.7 134.9 reduce-scatter.8
  694.2 134.5 reduce-scatter.10
where the time goes:
time: 845 us; the launch traced here: 836 us
  waiting for transfers between devices  358 us (42%)
  matrix products  235 us (28%)
  blocking collectives  85.2 us (10%)
  local copies, waits for them, and re-layouts  80.6 us (10%)
  other arithmetic  60.7 us (7%)
  between operations  15 us (2%)
    reduce_scatter x1, waiting for transfers between devices, local(): lax.psum_scatter(down_grad, ('gx', 'gy'), scatter_dimension=0, tiled=True)  142 us
    reduce_scatter x1, waiting for transfers between devices, local(): lax.psum_scatter(up_grad, ('gx', 'gy'), scatter_dimension=0, tiled=True)  141 us
    unnamed x2, blocking collectives  85.2 us
    dot_general x1, matrix products, local(): jnp.dot(normed_two, up_weight, preferred_element_type=jnp.float32)  38.2 us
    dot_general x4, matrix products, head_scores(): jnp.einsum('qhd,khd->hqk', split_heads(queries), split_heads(keys_all), p...  31.3 us
    all_gather x1, waiting for transfers between devices, local(): lax.all_gather(w_down, ('gx', 'gy'), axis=0, tiled=True)  27.2 us
    convert_element_type x2, other arithmetic, attend_backward(): grad_scores = (probs * (grad_probs - inner)).astype(jnp.bfloat16)  22.6 us
    dot_general x2, matrix products, attend_backward(): jnp.einsum('qhd,khd->hqk', grad_heads, split_heads(values_all), preferred...  21.3 us
  transfers between devices with their start and end apart: 8, of which 6 were waited for; matrix products, arithmetic and copies ran while one was open for 40% of the time, Pallas kernels for 0%

commit v1 on v0

--- a/solution.py
+++ b/solution.py
@@ -3,6 +3,8 @@
 import jax
 import jax.numpy as jnp
 from jax import lax
+from jax.experimental import pallas as pl
+from jax.experimental.pallas import tpu as pltpu
 from jax.sharding import PartitionSpec as P
 
 HEAD_DIM = 64
@@ -84,7 +86,461 @@
     return joined.astype(jnp.bfloat16)
 
 
+MESH = pl.DeviceIdType.MESH
+ANY = pl.ANY
+
+
+def gray(v):
+    return v + (v // 2) * (1 - 2 * (v % 2))
+
+
+class Place:
+    def __init__(self):
+        gx, gy = lax.axis_index("gx"), lax.axis_index("gy")
+        self.y, self.c, self.z, self.x = gx // 2, gx % 2, gy // 2, gy % 2
+        y, c, z, x = self.y, self.c, self.z, self.x
+        self.p = gray(z)
+        self.own = (y, x)
+        self.first = (y + c * (1 - 2 * y), x + (1 - c) * (1 - 2 * x))
+        self.second = (y + (1 - c) * (1 - 2 * y), x + c * (1 - 2 * x))
+        self.far = (1 - y, 1 - x)
+        self.to_first = self.dev(self.first, c, z)
+        self.to_second = self.dev(self.second, c, z)
+        self.to_next = self.dev(self.own, c, gray((self.p + 1) % 4))
+        self.to_prev = self.dev(self.own, c, gray((self.p + 3) % 4))
+        self.to_sibling = self.dev(self.own, 1 - c, z)
+
+    def dev(self, yx, c, z):
+        return (yx[0] * 2 + c, z * 2 + yx[1])
+
+    def chip(self, back):
+        return gray((self.p + 4 - back) % 4)
+
+    def greet(self):
+        barrier = pltpu.get_barrier_semaphore()
+        peers = (self.to_first, self.to_second, self.to_next, self.to_prev, self.to_sibling)
+        for peer in peers:
+            pl.semaphore_signal(barrier, inc=1, device_id=peer, device_id_type=MESH)
+        pl.semaphore_wait(barrier, len(peers))
+
+
+class Gather:
+    STAGES = 8
+
+    def __init__(self, place, src, dst, send, recv, here):
+        self.at, self.src, self.dst, self.send, self.recv, self.here = place, src, dst, send, recv, here
+
+    def column(self, yx):
+        return self.dst.at[yx[0], self.at.c, :, yx[1]]
+
+    def remote(self, k, src, dst, device):
+        return pltpu.make_async_remote_copy(
+            src_ref=src, dst_ref=dst, send_sem=self.send.at[k], recv_sem=self.recv.at[k],
+            device_id=device, device_id_type=MESH)
+
+    def ring(self, k):
+        a = self.at
+        block = self.dst.at[a.y, a.c, a.chip(k), a.x]
+        return self.remote(k, self.src if k == 0 else block, block, a.to_next)
+
+    def first(self):
+        col = self.column(self.at.own)
+        return self.remote(3, col, col, self.at.to_first)
+
+    def second(self, k):
+        col = self.column(self.at.own if k == 0 else self.at.first)
+        return self.remote(4 + k, col, col, self.at.to_second)
+
+    def twin(self, k):
+        a = self.at
+        col = self.column((a.own, a.first, a.second, a.far)[k])
+        return self.remote(6 + k, col, col, a.to_sibling)
+
+    def local(self):
+        a = self.at
+        return pltpu.make_async_copy(self.src, self.dst.at[a.y, a.c, a.z, a.x], self.here)
+
+    def stage(self, s):
+        if s == 0:
+            self.local().start()
+            self.ring(0).start()
+        elif s in (1, 2):
+            self.ring(s - 1).wait_recv()
+            self.ring(s).start()
+        elif s == 3:
+            self.local().wait()
+            self.ring(2).wait_recv()
+            self.first().start()
+            self.second(0).start()
+            self.twin(0).start()
+        elif s == 4:
+            self.first().wait_recv()
+            self.second(1).start()
+            self.twin(1).start()
+        elif s == 5:
+            self.second(0).wait_recv()
+            self.twin(2).start()
+        elif s == 6:
+            self.second(1).wait_recv()
+            self.twin(3).start()
+        elif s == 7:
+            for k in range(4):
+                self.twin(k).wait_recv()
+
+    def finish(self):
+        for k in range(3):
+            self.ring(k).wait_send()
+        self.first().wait_send()
+        self.second(0).wait_send()
+        self.second(1).wait_send()
+        for k in range(4):
+            self.twin(k).wait_send()
+
+
+def run_stages(jobs, offsets):
+    last = max(o + j.STAGES for j, o in zip(jobs, offsets))
+    for t in range(last):
+        for job, o in zip(jobs, offsets):
+            if 0 <= t - o < job.STAGES:
+                job.stage(t - o)
+    for job in jobs:
+        job.finish()
+
+
+def gather_all(shards, offsets):
+    n = len(shards)
+
+    def body(*refs):
+        src, dst = refs[:n], refs[n:2 * n]
+        send, recv, here = refs[2 * n:]
+        place = Place()
+        place.greet()
+        jobs = [Gather(place, src[i], dst[i], send.at[i], recv.at[i], here.at[i]) for i in range(n)]
+        run_stages(jobs, offsets)
+
+    return pl.pallas_call(
+        body,
+        out_shape=[jax.ShapeDtypeStruct((2, 2, 4, 2) + s.shape, s.dtype) for s in shards],
+        in_specs=[pl.BlockSpec(memory_space=ANY)] * n,
+        out_specs=[pl.BlockSpec(memory_space=ANY)] * n,
+        scratch_shapes=[pltpu.SemaphoreType.DMA((n, 10)), pltpu.SemaphoreType.DMA((n, 10)), pltpu.SemaphoreType.DMA((n,))],
+        compiler_params=pltpu.CompilerParams(collective_id=0, has_side_effects=True),
+        name="gather_weights",
+    )(*shards)
+
+
+class Scatter:
+    STAGES = 9
+
+    def __init__(self, place, src, out, held, twin, side, end, rings, send, recv, here):
+        self.at, self.src, self.out = place, src, out
+        self.held, self.twin, self.side, self.end, self.rings = held, twin, side, end, rings
+        self.send, self.recv, self.here = send, recv, here
+
+    def remote(self, k, src, dst, device):
+        return pltpu.make_async_remote_copy(
+            src_ref=src, dst_ref=dst, send_sem=self.send.at[k], recv_sem=self.recv.at[k],
+            device_id=device, device_id_type=MESH)
+
+    def load(self, k):
+        a = self.at
+        yx = (a.far, a.second, a.first, a.own)[k]
+        return pltpu.make_async_copy(self.src.at[yx[0], a.c, :, yx[1]], self.held.at[k], self.here.at[k])
+
+    def to_twin(self, k):
+        a = self.at
+        yx = (a.far, a.first, a.second, a.own)[k]
+        return self.remote(k, self.src.at[yx[0], 1 - a.c, :, yx[1]], self.twin.at[k], a.to_sibling)
+
+    def to_second(self, k):
+        return self.remote(4 + k, self.held.at[k], self.side.at[k], self.at.to_second)
+
+    def to_first(self):
+        return self.remote(6, self.held.at[2], self.end, self.at.to_first)
+
+    def ring(self, k):
+        return self.remote(7 + k, self.held.at[3, self.at.chip(k + 1)], self.rings.at[k], self.at.to_next)
+
+    def add(self, k, other):
+        held = self.held
+
+        def one(z, carry):
+            total = held[k, z].astype(jnp.float32) + other[z].astype(jnp.float32)
+            held[k, z] = total.astype(held.dtype)
+            return carry
+
+        lax.fori_loop(0, 4, one, 0)
+
+    def stage(self, s):
+        a = self.at
+        if s == 0:
+            for k in range(4):
+                self.load(k).start()
+                self.to_twin(k).start()
+        elif s == 1:
+            for k in range(2):
+                self.load(k).wait()
+                self.to_twin(k).wait_recv()
+                self.add(k, self.twin.at[k])
+                self.to_second(k).start()
+        elif s == 2:
+            for k in (2, 3):
+                self.load(k).wait()
+                self.to_twin(k).wait_recv()
+                self.add(k, self.twin.at[k])
+        elif s == 3:
+            self.to_second(0).wait_recv()
+            self.add(2, self.side.at[0])
+            self.to_first().start()
+        elif s == 4:
+            self.to_second(1).wait_recv()
+            self.add(3, self.side.at[1])
+        elif s == 5:
+            self.to_first().wait_recv()
+            self.add(3, self.end)
+            self.ring(0).start()
+        elif s in (6, 7):
+            self.ring(s - 6).wait_recv()
+            z = a.chip(s - 4)
+            total = self.held[3, z].astype(jnp.float32) + self.rings[s - 6].astype(jnp.float32)
+            self.held[3, z] = total.astype(self.held.dtype)
+            self.ring(s - 5).start()
+        elif s == 8:
+            self.ring(2).wait_recv()
+            self.out[...] = self.held[3, a.z].astype(jnp.float32) + self.rings[2].astype(jnp.float32)
+
+    def finish(self):
+        for k in range(4):
+            self.to_twin(k).wait_send()
+        self.to_second(0).wait_send()
+        self.to_second(1).wait_send()
+        self.to_first().wait_send()
+        for k in range(3):
+            self.ring(k).wait_send()
+
+
+def scatter_scratch(rows, cols, dtype):
+    return [pltpu.VMEM((4, 4, rows, cols), dtype), pltpu.VMEM((4, 4, rows, cols), dtype),
+            pltpu.VMEM((2, 4, rows, cols), dtype), pltpu.VMEM((4, rows, cols), dtype),
+            pltpu.VMEM((3, rows, cols), dtype)]
+
+
+def scatter_all(partials, offsets):
+    n = len(partials)
+
+    def body(*refs):
+        src, out = refs[:n], refs[n:2 * n]
+        scratch = refs[2 * n:7 * n]
+        send, recv, here = refs[7 * n:]
+        place = Place()
+        place.greet()
+        jobs = [Scatter(place, src[i], out[i], *scratch[5 * i:5 * i + 5], send.at[i], recv.at[i], here.at[i]) for i in range(n)]
+        run_stages(jobs, offsets)
+
+    scratch = []
+    for p in partials:
+        scratch += scatter_scratch(*p.shape[4:], p.dtype)
+    return pl.pallas_call(
+        body,
+        out_shape=[jax.ShapeDtypeStruct(p.shape[4:], jnp.float32) for p in partials],
+        in_specs=[pl.BlockSpec(memory_space=ANY)] * n,
+        out_specs=[pl.BlockSpec(memory_space=pltpu.VMEM)] * n,
+        scratch_shapes=scratch + [pltpu.SemaphoreType.DMA((n, 10)), pltpu.SemaphoreType.DMA((n, 10)), pltpu.SemaphoreType.DMA((n, 4))],
+        compiler_params=pltpu.CompilerParams(collective_id=1, has_side_effects=True, vmem_limit_bytes=50 << 20),
+        name="scatter_grads",
+    )(*partials)
+
+def pack_vectors(eight, wide):
+    block = jnp.stack(eight, axis=-2)
+    rows = wide.reshape(wide.shape[:-1] + (4, -1))
+    lead = [(0, 0)] * (block.ndim - 2)
+    rows = jnp.pad(rows, lead + [(0, 4), (0, 0)])
+    joined = jnp.concatenate([block, rows], axis=-1)
+    return jnp.pad(joined, lead + [(0, 0), (0, 128 - joined.shape[-1])])
+
+
+def unpack_vectors(blocks, share):
+    eight = tuple(blocks[:, k, :share].reshape(-1) for k in range(8))
+    return eight, blocks[:, :4, share : 2 * share].reshape(-1)
+
+
 def local(
+    patches,
+    cotangent,
+    counts,
+    blank_mask,
+    ln1_gain,
+    ln1_shift,
+    w_qkv,
+    query_bias,
+    value_bias,
+    w_proj,
+    proj_bias,
+    ln2_gain,
+    ln2_shift,
+    w_up,
+    up_bias,
+    w_down,
+    down_bias,
+):
+    items_here = counts.shape[0]
+    length = blank_mask.shape[1]
+    width = patches.shape[1]
+    positions = jnp.arange(length, dtype=jnp.int32)
+    live_mask = positions[None, :] < counts[:, None]
+    allowed = live_mask & ((blank_mask == 1) | (positions[None, :] == 0))
+    live_rows = live_mask.reshape(-1, 1).astype(jnp.float32)
+    vectors = pack_vectors(
+        (ln1_gain, ln1_shift, query_bias, value_bias, proj_bias, ln2_gain, ln2_shift, down_bias),
+        up_bias,
+    )
+    all_qkv, all_vectors, all_proj, all_up, all_down = gather_all(
+        (w_qkv, vectors, w_proj, w_up, w_down), (0, 0, 3, 4, 7)
+    )
+    qkv_weight = all_qkv.reshape(width, -1)
+    proj_weight = all_proj.reshape(width, width)
+    up_weight = all_up.reshape(width, -1)
+    down_weight = all_down.reshape(-1, width)
+    (
+        gain_one,
+        shift_one,
+        bias_query,
+        bias_value,
+        bias_proj,
+        gain_two,
+        shift_two,
+        bias_down,
+    ), bias_up = unpack_vectors(all_vectors.reshape(-1, 8, 128), w_qkv.shape[0])
+    inputs = patches.astype(jnp.float32)
+    gain_float = gain_one.astype(jnp.float32)
+    shift_float = shift_one.astype(jnp.float32)
+    normed_low = normalize(inputs, gain_float, shift_float).astype(jnp.bfloat16)
+    projected = jnp.dot(normed_low, qkv_weight, preferred_element_type=jnp.float32)
+    queries = (projected[:, :width] + bias_query.astype(jnp.float32)).astype(jnp.bfloat16)
+    keys_all = projected[:, width : 2 * width].astype(jnp.bfloat16)
+    values_all = (projected[:, 2 * width :] + bias_value.astype(jnp.float32)).astype(jnp.bfloat16)
+    per_item = (
+        queries.reshape(items_here, length, width),
+        keys_all.reshape(items_here, length, width),
+        values_all.reshape(items_here, length, width),
+        allowed,
+    )
+    mixed_items, log_totals = lax.map(attend_forward, per_item)
+    mixed_low = mixed_items.reshape(-1, width)
+    residual = (
+        inputs
+        + jnp.dot(mixed_low, proj_weight, preferred_element_type=jnp.float32)
+        + bias_proj.astype(jnp.float32)
+    )
+    normed_two = normalize(
+        residual, gain_two.astype(jnp.float32), shift_two.astype(jnp.float32)
+    ).astype(jnp.bfloat16)
+    pre_act = jnp.dot(normed_two, up_weight, preferred_element_type=jnp.float32) + bias_up.astype(
+        jnp.float32
+    )
+    activated, gelu_back = jax.vjp(partial(jax.nn.gelu, approximate=False), pre_act)
+    act_low = activated.astype(jnp.bfloat16)
+    out_branch = jnp.dot(
+        act_low, down_weight, preferred_element_type=jnp.float32
+    ) + bias_down.astype(jnp.float32)
+    output = ((residual + out_branch) * live_rows).astype(jnp.bfloat16)
+    grad_out = cotangent.astype(jnp.float32) * live_rows
+    grad_down_low = grad_out.astype(jnp.bfloat16)
+    down_grad = jnp.einsum("tf,td->fd", act_low, grad_down_low, preferred_element_type=jnp.float32)
+    down_bias_grad = jnp.sum(grad_down_low.astype(jnp.float32), axis=0)
+    grad_act = jnp.einsum(
+        "td,fd->tf", grad_down_low, down_weight, preferred_element_type=jnp.float32
+    )
+    grad_pre_low = gelu_back(grad_act)[0].astype(jnp.bfloat16)
+    up_grad = jnp.einsum("td,tf->df", normed_two, grad_pre_low, preferred_element_type=jnp.float32)
+    up_bias_grad = jnp.sum(grad_pre_low.astype(jnp.float32), axis=0)
+    grad_normed_two = jnp.einsum(
+        "tf,df->td", grad_pre_low, up_weight, preferred_element_type=jnp.float32
+    )
+    _, norm_back_two = jax.vjp(
+        normalize, residual, gain_two.astype(jnp.float32), shift_two.astype(jnp.float32)
+    )
+    grad_resid_part, gain_two_grad, shift_two_grad = norm_back_two(grad_normed_two)
+    grad_resid = grad_out + grad_resid_part
+    grad_branch_low = grad_resid.astype(jnp.bfloat16)
+    proj_grad = jnp.einsum(
+        "td,te->de", mixed_low, grad_branch_low, preferred_element_type=jnp.float32
+    )
+    proj_bias_grad = jnp.sum(grad_branch_low.astype(jnp.float32), axis=0)
+    grad_mixed = jnp.einsum(
+        "te,de->td", grad_branch_low, proj_weight, preferred_element_type=jnp.float32
+    ).astype(jnp.bfloat16)
+    back_items = (
+        per_item[0],
+        per_item[1],
+        per_item[2],
+        allowed,
+        log_totals,
+        grad_mixed.reshape(items_here, length, width),
+    )
+    grad_projected = lax.map(attend_backward, back_items).reshape(-1, 3 * width)
+    qkv_grad = jnp.einsum(
+        "td,te->de", normed_low, grad_projected, preferred_element_type=jnp.float32
+    )
+    query_bias_grad = jnp.sum(grad_projected[:, :width].astype(jnp.float32), axis=0)
+    value_bias_grad = jnp.sum(grad_projected[:, 2 * width :].astype(jnp.float32), axis=0)
+    grad_normed = jnp.einsum(
+        "te,de->td", grad_projected, qkv_weight, preferred_element_type=jnp.float32
+    )
+    _, norm_back_one = jax.vjp(
+        normalize, inputs, gain_one.astype(jnp.float32), shift_one.astype(jnp.float32)
+    )
+    grad_input_part, gain_one_grad, shift_one_grad = norm_back_one(grad_normed)
+    grad_input = (grad_resid + grad_input_part).astype(jnp.bfloat16)
+    packed = pack_vectors(
+        tuple(
+            v.reshape(-1, w_qkv.shape[0])
+            for v in (
+                gain_one_grad,
+                shift_one_grad,
+                query_bias_grad,
+                value_bias_grad,
+                proj_bias_grad,
+                gain_two_grad,
+                shift_two_grad,
+                down_bias_grad,
+            )
+        ),
+        up_bias_grad.reshape(-1, up_bias.shape[0]),
+    )
+    low = jnp.bfloat16
+    blocks = tuple(
+        t.reshape((2, 2, 4, 2) + s)
+        for t, s in (
+            (down_grad.astype(low), w_down.shape),
+            (up_grad.astype(low), w_up.shape),
+            (proj_grad.astype(low), w_proj.shape),
+            (qkv_grad.astype(low), w_qkv.shape),
+            (packed, (8, 128)),
+        )
+    )
+    own_down, own_up, own_proj, own_qkv, own_packed = scatter_all(blocks, (0, 3, 6, 7, 8))
+    own_vectors, own_up_bias = unpack_vectors(own_packed[None], w_qkv.shape[0])
+    return (
+        output,
+        grad_input,
+        own_vectors[0],
+        own_vectors[1],
+        own_qkv,
+        own_vectors[2],
+        own_vectors[3],
+        own_proj,
+        own_vectors[4],
+        own_vectors[5],
+        own_vectors[6],
+        own_up,
+        own_up_bias,
+        own_down,
+        own_vectors[7],
+    )
+
+
+def plain_local(
     patches,
     cotangent,
     counts,
@@ -294,8 +750,9 @@
         P(("gx", "gy"), None),
         P(("gx", "gy")),
     )
+    mine = dict(mesh.shape) == {"gx": 4, "gy": 8}
     return jax.shard_map(
-        local,
+        local if mine else plain_local,
         mesh=mesh,
         in_specs=placed,
         out_specs=(

time: 845 us -> 555 us (0.66)
  waiting for transfers between devices: 358 us -> 0 us
  Pallas kernels: 0 us -> 182 us
  blocking collectives: 85.2 us -> 0 us
  matrix products: 235 us -> 218 us
  between operations: 15 us -> 1.89 us
    reduce_scatter x4 -> x0, waiting for transfers between devices: 297 us -> none  [the longest x1 142 us: local(): lax.psum_scatter(down_grad, ('gx', 'gy'), scatter_dimension=0, tiled=True)]
    pallas_call x0 -> x2, Pallas kernels: none -> 182 us  [the longest x1 92.9 us: gather_all(): pl.pallas_call(body, out_shape=[jax.ShapeDtypeStruct((2, 2, 4, 2) + s.sha...]
    unnamed x2 -> x0, blocking collectives: 85.2 us -> none
    all_gather x4 -> x0, waiting for transfers between devices: 58.1 us -> none  [the longest x1 27.2 us: local(): lax.all_gather(w_down, ('gx', 'gy'), axis=0, tiled=True)]
    unnamed x113 -> x100, local copies, waits for them, and re-layouts: 18.9 us -> 4.18 us
  transfers between devices with their start and end apart: 8 -> 0, of which waited for: 6 -> 0; matrix products, arithmetic and copies ran while one was open for 40% -> 0% of each run, Pallas kernels for 0% -> 0%
where the time goes in v1:
time: 555 us; the launch traced here: 546 us
  matrix products  218 us (39%)
  Pallas kernels  182 us (33%)
  local copies, waits for them, and re-layouts  77.6 us (14%)
  other arithmetic  65.7 us (12%)
    pallas_call x1, Pallas kernels, gather_all(): pl.pallas_call(body, out_shape=[jax.ShapeDtypeStruct((2, 2, 4, 2) + s.sha...  92.9 us
    pallas_call x1, Pallas kernels, scatter_all(): pl.pallas_call(body, out_shape=[jax.ShapeDtypeStruct(p.shape[4:], jnp.flo...  89.5 us
    dot_general x1, matrix products, local(): jnp.dot(normed_two, up_weight, preferred_element_type=jnp.float32)  35.7 us
    dot_general x4, matrix products, head_scores(): jnp.einsum('qhd,khd->hqk', split_heads(queries), split_heads(keys_all), p...  31 us
    convert_element_type x2, other arithmetic, attend_backward(): grad_scores = (probs * (grad_probs - inner)).astype(jnp.bfloat16)  22.4 us
    dot_general x2, matrix products, attend_forward(): jnp.einsum('hqk,khd->qhd', probs.astype(jnp.bfloat16), split_heads(values...  21.1 us
    dot_general x2, matrix products, attend_backward(): jnp.einsum('qhd,khd->hqk', grad_heads, split_heads(values_all), preferred...  21.1 us
    reduce_sum x2, other arithmetic, attend_forward(): jnp.sum(jnp.exp(masked - peak), axis=-1, keepdims=True)  18.3 us

profile of v1, /device:TPU:0, one launch (start us, length us, event | category | flops | bytes accessed | tf_op | source)
XLA Modules:
  0.0 546.0 jit_solution(12424333615143110556)
XLA Ops:
  6.2 2.1 fusion.30
  8.3 92.9 %gather_weights.1 = (bf16[2,2,4,2,24,2304]{5,4,3,2,1,0:T(8,128)(2,1)}, bf16[2,2,4,2,8,128]{5,4,3,2,1,0:T(8,128)(2,1)}, bf16[2,2,4,2,24,768]{5,4,3,2,1,0:T(8,128)...) custom-call(bf16[24,2304]{1,0:T(8,128)(2,1)} %refs_0_.1, bf16[8,128]{1,0:T(8,128)(2,1)} %pad.17.refs_1_, ...), custom_call_target="tpu_custom_call" | custom-call | tf_op jit(solution)/shard_map/gather_weights/pallas_call | solution.py:221
  106.0 6.4 %fusion.51 = f32[1058,2304]{1,0:T(8,128)S(1)} fusion(bf16[768,2304]{1,0:T(8,128)(2,1)} %bitcast.178, bf16[1058,768]{1,0:T(8,128)(2,1)S(1)} %copy-done.3, f32[768]{0:T(1024)S(1)} %reshape.379, f32[768]{0:T(1024)S(1)} %reshape.378, f32[1058]{0:T(1024)S(1)} %fusion.43, f32[1058]{0:T(1024)S(1)} %broadcast_multiply_fusion.1), kind=kOutput, calls=%fused_computation.146 | convolution fusion | flops 3749078016 | bytes 14929168 | tf_op jit(solution)/shard_map/dot_general | solution.py:418
  112.5 1.8 fusion.32
  117.3 2.9 copy.49
  120.2 3.9 copy.48
  124.1 2.9 reshape.363
  127.0 3.8 copy.47
  130.8 65.4 %while.22 = (s32[]{:T(128)}, bf16[2,529,768]{2,1,0:T(8,128)(2,1)}, f32[2,12,529,1]{2,1,3,0:T(8,128)S(1)}, bf16[2,529,768]{1,2,0:T(8,128)(2,1)}, pred[2,529]{1,0:...) while((s32[]{:T(128)}, bf16[2,529,768]{2,1,0:T(8,128)(2,1)}, ...), condition=%wide.region_5.6_spmd, body=%wide.region_2.5_spmd.sunk | while | flops 897010432 | bytes 51951636 | solution.py:428
  133.6 7.6 %fusion.108 = (f32[12,529]{1,0:T(8,128)S(1)}, f32[12,529,529]{1,2,0:T(8,128)}) fusion(pred[529]{0:T(1024)(128)(4,1)S(1)} %dynamic-slice_reduce_fusion.4, bf16[529,12,64]{0,2,1:T(8,128)(2,1)S(1)} %bitcast.154, bf16[529,12,64]{0,2,1:T(8,128)(2,1)S(1)} %bitcast.153), kind=kOutput, calls=%fused_computation.3.clone.1 | convolution fusion | flops 439903680 | bytes 15083377 | tf_op jit(solution)/shard_map/while/body/eval_jaxpr/qhd,khd->hqk/dot_general | solution.py:28
  141.2 9.2 %exponential_reduce_fusion.2 = f32[12,529]{1,0:T(8,128)S(1)} fusion(f32[12,529,529]{1,2,0:T(8,128)} %get-tuple-element.326, f32[12,529]{1,0:T(8,128)S(1)} %get-tuple-element.327, pred[529]{0:T(1024)(128)(4,1)S(1)} %dynamic-slice_reduce_fusion.4), kind=kLoop, calls=%fused_computation.1.clone.1 | loop fusion | flops 13426020 | bytes 13483681 | tf_op jit(solution)/shard_map/while/body/eval_jaxpr/reduce_sum | solution.py:41
  150.4 10.5 %fusion.109 = bf16[12,64,529]{2,1,0:T(8,128)(2,1)} fusion(bf16[529,12,64]{0,2,1:T(8,128)(2,1)S(1)} %bitcast.157, f32[12,529,529]{1,2,0:T(8,128)} %get-tuple-element.326, f32[12,529]{1,0:T(8,128)S(1)} %get-tuple-element.328, pred[529]{0:T(1024)(128)(4,1)S(1)} %dynamic-slice_reduce_fusion.4), kind=kOutput, calls=%fused_computation.6.clone.1 | convolution fusion | flops 443674432 | bytes 15083377 | tf_op jit(solution)/shard_map/while/body/eval_jaxpr/hqk,khd->qhd/dot_general | solution.py:43
  166.2 7.6 %fusion.108 = (f32[12,529]{1,0:T(8,128)S(1)}, f32[12,529,529]{1,2,0:T(8,128)}) fusion(pred[529]{0:T(1024)(128)(4,1)S(1)} %dynamic-slice_reduce_fusion.4, bf16[529,12,64]{0,2,1:T(8,128)(2,1)S(1)} %bitcast.154, bf16[529,12,64]{0,2,1:T(8,128)(2,1)S(1)} %bitcast.153), kind=kOutput, calls=%fused_computation.3.clone.1 | convolution fusion | flops 439903680 | bytes 15083377 | tf_op jit(solution)/shard_map/while/body/eval_jaxpr/qhd,khd->hqk/dot_general | solution.py:28
  173.8 9.2 %exponential_reduce_fusion.2 = f32[12,529]{1,0:T(8,128)S(1)} fusion(f32[12,529,529]{1,2,0:T(8,128)} %get-tuple-element.326, f32[12,529]{1,0:T(8,128)S(1)} %get-tuple-element.327, pred[529]{0:T(1024)(128)(4,1)S(1)} %dynamic-slice_reduce_fusion.4), kind=kLoop, calls=%fused_computation.1.clone.1 | loop fusion | flops 13426020 | bytes 13483681 | tf_op jit(solution)/shard_map/while/body/eval_jaxpr/reduce_sum | solution.py:41
  183.1 10.5 %fusion.109 = bf16[12,64,529]{2,1,0:T(8,128)(2,1)} fusion(bf16[529,12,64]{0,2,1:T(8,128)(2,1)S(1)} %bitcast.157, f32[12,529,529]{1,2,0:T(8,128)} %get-tuple-element.326, f32[12,529]{1,0:T(8,128)S(1)} %get-tuple-element.328, pred[529]{0:T(1024)(128)(4,1)S(1)} %dynamic-slice_reduce_fusion.4), kind=kOutput, calls=%fused_computation.6.clone.1 | convolution fusion | flops 443674432 | bytes 15083377 | tf_op jit(solution)/shard_map/while/body/eval_jaxpr/hqk,khd->qhd/dot_general | solution.py:43
  196.3 3.7 reshape.366
  200.0 4.0 fusion.58
  205.6 35.7 %multiply_convert_fusion.3 = (bf16[1058,3072]{1,0:T(8,128)(2,1)}, f32[1058,3072]{1,0:T(8,128)}, f32[1058,3072]{1,0:T(8,128)}) fusion(f32[3072]{0:T(1024)S(1)} %reshape.385, bf16[768,3072]{1,0:T(8,128)(2,1)S(1)} %bitcast.174, f32[1058,768]{1,0:T(8,128)S(1)} %get-tuple-element.224, f32[768]{0:T(1024)S(1)} %reshape.384, f32[768]{0:T(1024)S(1)} %reshape.383, ...), kind=kOutput, calls=%fused_computation.37 | convolution fusion | flops 5210844672 | bytes 40497424 | tf_op jit(solution)/shard_map/dot_general | solution.py:438
  241.4 17.2 %convert_reduce_fusion = (f32[3072]{0:T(1024)S(1)}, bf16[1058,3072]{1,0:T(8,128)(2,1)}) fusion(f32[1058,3072]{1,0:T(8,128)} %get-tuple-element.201, f32[1058,3072]{1,0:T(8,128)} %get-tuple-element.225, bf16[3072,768]{1,0:T(8,128)(2,1)} %bitcast.176, bf16[1058,768]{1,0:T(8,128)(2,1)} %param.22, f32[1058]{0:T(1024)S(1)} %copy-done.24), kind=kOutput, calls=%fused_computation.35 | convolution fusion | flops 5046707712 | bytes 38861960 | tf_op jit(solution)/shard_map/td,fd->tf/dot_general | solution.py:451
  258.6 10.3 %fusion.26 = bf16[1058,768]{1,0:T(8,128)(2,1)} fusion(f32[1058,768]{1,0:T(8,128)S(1)} %copy-done.7, bf16[1058,3072]{1,0:T(8,128)(2,1)} %get-tuple-element.200, bf16[3072,768]{1,0:T(8,128)(2,1)} %bitcast.177, f32[1058]{0:T(1024)S(1)} %copy-done.24, f32[768]{0:T(1024)S(1)} %copy-done.38), kind=kOutput, calls=%fused_computation.70 | convolution fusion | flops 4995520512 | bytes 16101512 | tf_op jit(solution)/shard_map/dot_general | solution.py:443
  269.0 9.0 %convolution_convert_fusion.2 = bf16[3072,768]{1,0:T(8,128)(2,1)} fusion(bf16[1058,3072]{1,0:T(8,128)(2,1)S(1)} %copy-done.41, bf16[1058,768]{1,0:T(8,128)(2,1)S(1)} %copy-done.9, f32[1058]{0:T(1024)S(1)} %copy-done.24), kind=kOutput, calls=%fused_computation.53 | convolution fusion | flops 4997067264 | bytes 12848264 | tf_op jit(solution)/shard_map/tf,td->fd/dot_general | solution.py:449
  278.0 6.0 %multiply_reduce_fusion.1 = (f32[768]{0:T(1024)S(1)}, f32[1058]{0:T(1024)S(1)}, f32[768]{0:T(1024)S(1)}, f32[1058,768]{1,0:T(8,128)S(1)}) fusion(f32[1058,768]{1,0:T(8,128)S(1)} %copy-done.7, f32[1058]{0:T(1024)S(1)} %fusion.44, f32[1058]{0:T(1024)S(1)} %broadcast_multiply_fusion, f32[768]{0:T(1024)S(1)} %reshape.383, ...), kind=kOutput, calls=%fused_computation.82 | convolution fusion | flops 4998767616 | bytes 17741208 | tf_op jit(solution)/shard_map/tf,df->td/dot_general | solution.py:457
  285.2 8.7 %convolution_convert_fusion.1 = bf16[768,3072]{1,0:T(8,128)(2,1)} fusion(bf16[1058,3072]{1,0:T(8,128)(2,1)S(1)} %copy-done.40, f32[1058,768]{1,0:T(8,128)S(1)} %copy-done.8, f32[768]{0:T(1024)S(1)} %reshape.384, f32[768]{0:T(1024)S(1)} %reshape.383, f32[1058]{0:T(1024)S(1)} %fusion.44, f32[1058]{0:T(1024)S(1)} %broadcast_multiply_fusion), kind=kOutput, calls=%fused_computation.52 | convolution fusion | flops 4998692352 | bytes 14483728 | tf_op jit(solution)/shard_map/td,tf->df/dot_general | solution.py:455
  296.1 2.3 convert_reduce_fusion.3
  301.6 3.2 convolution_convert_fusion.3
  306.4 114.4 %while.23 = (s32[]{:T(128)}, bf16[2,529,2304]{2,1,0:T(8,128)(2,1)}, bf16[2,529,768]{1,2,0:T(8,128)(2,1)}, pred[2,529]{1,0:T(4,128)(4,1)S(1)}, bf16[2,529,768]{1,...) while((s32[]{:T(128)}, bf16[2,529,2304]{2,1,0:T(8,128)(2,1)}, ...), condition=%wide.region_12.13_spmd, body=%wide.region_10.12_spmd.sunk | while | flops 2188739584 | bytes 131812608 | solution.py:481
  311.5 7.9 %subtract_exponential_fusion.2 = f32[12,529,529]{1,2,0:T(8,128)} fusion(bf16[529,12,64]{0,2,1:T(8,128)(2,1)S(1)} %bitcast.150, bf16[529,12,64]{0,2,1:T(8,128)(2,1)S(1)} %bitcast.146, f32[12,529]{1,0:T(8,128)S(1)} %dynamic-slice_bitcast_fusion.2, pred[529]{0:T(1024)(128)(4,1)S(1)} %dynamic-slice_reduce_fusion.5), kind=kOutput, calls=%fused_computation.18.clone.1 | convolution fusion | flops 439910016 | bytes 15083377 | tf_op jit(solution)/shard_map/while/body/eval_jaxpr/qhd,khd->hqk/dot_general | solution.py:28
  319.4 8.4 %fusion.120 = bf16[12,64,529]{2,1,0:T(8,128)(2,1)S(1)} fusion(bf16[529,12,64]{0,2,1:T(8,128)(2,1)S(1)} %bitcast.144, f32[12,529,529]{1,2,0:T(8,128)} %subtract_exponential_fusion.2), kind=kOutput, calls=%fused_computation.24.clone.1 | convolution fusion | flops 433600128 | bytes 15057456 | tf_op jit(solution)/shard_map/while/body/eval_jaxpr/hqk,qhd->khd/dot_general | solution.py:75
  327.7 10.5 %multiply_reduce_fusion.5 = (f32[12,529]{1,0:T(8,128)S(1)}, f32[12,529,529]{1,2,0:T(8,128)}) fusion(f32[12,529,529]{1,2,0:T(8,128)} %subtract_exponential_fusion.2, bf16[529,12,64]{0,2,1:T(8,128)(2,1)S(1)} %bitcast.145, bf16[529,12,64]{0,2,1:T(8,128)(2,1)S(1)} %bitcast.152), kind=kOutput, calls=%fused_computation.17.clone.1 | convolution fusion | flops 436545600 | bytes 28515216 | tf_op jit(solution)/shard_map/while/body/eval_jaxpr/qhd,khd->hqk/dot_general | solution.py:57
  338.3 11.2 %multiply_convert_fusion.7 = bf16[12,529,529]{1,2,0:T(8,128)(2,1)S(1)} fusion(f32[12,529,529]{1,2,0:T(8,128)} %subtract_exponential_fusion.2, f32[12,529,529]{1,2,0:T(8,128)} %get-tuple-element.340, f32[12,529]{1,0:T(8,128)S(1)} %get-tuple-element.341), kind=kLoop, calls=%fused_computation.16.clone.1 | loop fusion | flops 10074276 | bytes 33606312 | tf_op jit(solution)/shard_map/while/body/eval_jaxpr/convert_element_type | solution.py:61
  351.2 2.7 multiply_convert_fusion.8
  353.9 1.9 pad_maximum_fusion.2
  355.8 4.5 copy.78
  360.3 3.3 constant_dynamic-update-slice_fusion.13
  368.4 7.9 %subtract_exponential_fusion.2 = f32[12,529,529]{1,2,0:T(8,128)} fusion(bf16[529,12,64]{0,2,1:T(8,128)(2,1)S(1)} %bitcast.150, bf16[529,12,64]{0,2,1:T(8,128)(2,1)S(1)} %bitcast.146, f32[12,529]{1,0:T(8,128)S(1)} %dynamic-slice_bitcast_fusion.2, pred[529]{0:T(1024)(128)(4,1)S(1)} %dynamic-slice_reduce_fusion.5), kind=kOutput, calls=%fused_computation.18.clone.1 | convolution fusion | flops 439910016 | bytes 15083377 | tf_op jit(solution)/shard_map/while/body/eval_jaxpr/qhd,khd->hqk/dot_general | solution.py:28
  376.3 8.4 %fusion.120 = bf16[12,64,529]{2,1,0:T(8,128)(2,1)S(1)} fusion(bf16[529,12,64]{0,2,1:T(8,128)(2,1)S(1)} %bitcast.144, f32[12,529,529]{1,2,0:T(8,128)} %subtract_exponential_fusion.2), kind=kOutput, calls=%fused_computation.24.clone.1 | convolution fusion | flops 433600128 | bytes 15057456 | tf_op jit(solution)/shard_map/while/body/eval_jaxpr/hqk,qhd->khd/dot_general | solution.py:75
  384.7 10.5 %multiply_reduce_fusion.5 = (f32[12,529]{1,0:T(8,128)S(1)}, f32[12,529,529]{1,2,0:T(8,128)}) fusion(f32[12,529,529]{1,2,0:T(8,128)} %subtract_exponential_fusion.2, bf16[529,12,64]{0,2,1:T(8,128)(2,1)S(1)} %bitcast.145, bf16[529,12,64]{0,2,1:T(8,128)(2,1)S(1)} %bitcast.152), kind=kOutput, calls=%fused_computation.17.clone.1 | convolution fusion | flops 436545600 | bytes 28515216 | tf_op jit(solution)/shard_map/while/body/eval_jaxpr/qhd,khd->hqk/dot_general | solution.py:57
  395.2 11.2 %multiply_convert_fusion.7 = bf16[12,529,529]{1,2,0:T(8,128)(2,1)S(1)} fusion(f32[12,529,529]{1,2,0:T(8,128)} %subtract_exponential_fusion.2, f32[12,529,529]{1,2,0:T(8,128)} %get-tuple-element.340, f32[12,529]{1,0:T(8,128)S(1)} %get-tuple-element.341), kind=kLoop, calls=%fused_computation.16.clone.1 | loop fusion | flops 10074276 | bytes 33606312 | tf_op jit(solution)/shard_map/while/body/eval_jaxpr/convert_element_type | solution.py:61
  408.1 2.7 multiply_convert_fusion.8
  410.9 1.9 pad_maximum_fusion.2
  412.7 4.5 copy.78
  417.2 3.3 constant_dynamic-update-slice_fusion.13
  420.8 5.7 %reshape.371 = bf16[1058,2304]{1,0:T(8,128)(2,1)} reshape(bf16[2,529,2304]{2,1,0:T(8,128)(2,1)} %get-tuple-element.112) | data formatting | bytes 9750528 | tf_op jit(solution)/shard_map/reshape | solution.py:481
  426.5 9.5 %fusion.54 = (f32[768]{0:T(1024)S(1)}, f32[1058]{0:T(1024)S(1)}, f32[1058,768]{1,0:T(8,128)}) fusion(f32[768]{0:T(1024)S(1)} %copy-done.35, f32[1058]{0:T(1024)S(1)} %copy-done.19, bf16[1058,768]{1,0:T(8,128)(2,1)S(1)} %copy-done.4, bf16[1058,2304]{1,0:T(8,128)(2,1)} %reshape.371, bf16[768,2304]{1,0:T(8,128)(2,1)} %bitcast.179), kind=kOutput, calls=%fused_computation.148 | convolution fusion | flops 3749076224 | bytes 13304080 | tf_op jit(solution)/shard_map/te,de->td/dot_general | solution.py:487
  436.8 6.9 %convolution_convert_fusion = bf16[768,2304]{1,0:T(8,128)(2,1)} fusion(bf16[1058,2304]{1,0:T(8,128)(2,1)S(1)} %copy-done.5, bf16[1058,768]{1,0:T(8,128)(2,1)S(1)} %copy-done.4, f32[768]{0:T(1024)S(1)} %copy-done.37, f32[768]{0:T(1024)S(1)} %copy-done.35, f32[1058]{0:T(1024)S(1)} %copy-done.21, f32[1058]{0:T(1024)S(1)} %copy-done.19), kind=kOutput, calls=%fused_computation.51 | convolution fusion | flops 3750847488 | bytes 10053904 | tf_op jit(solution)/shard_map/td,te->de/dot_general | solution.py:482
  443.8 3.6 fusion.29
  447.5 4.1 add_convert_fusion.1
  452.1 89.5 %scatter_grads.1 = (f32[96,768]{1,0:T(8,128)S(1)}, f32[24,3072]{1,0:T(8,128)S(1)}, f32[24,768]{1,0:T(8,128)S(1)}, f32[24,2304]{1,0:T(8,128)S(1)}, f32[8,128]{1,0:T(8,128)S(1)}) custom-call(bf16[2,2,4,2,96,768]{5,4,3,2,1,0:T(8,128)(2,1)} %bitcast.158, bf16[2,2,4,2,24,3072]{5,4,3,2,1,0:T(8,128)(2,1)} %bitcast.159, ...), custom_call_target="tpu_custom_call" | custom-call | tf_op jit(solution)/shard_map/scatter_grads/pallas_call | solution.py:343
  (183 shorter events, 51.9 us)
Async XLA Ops:
  0.6 105.3 %copy-start.3 = (bf16[1058,768]{1,0:T(8,128)(2,1)S(1)}, bf16[1058,768]{1,0:T(8,128)(2,1)}, u32[]{:S(2)}) copy-start(bf16[1058,768]{1,0:T(8,128)(2,1)} %param.21) | copy-start | bytes 4875268
  6.2 106.2 %copy-start.18 = (f32[1058]{0:T(1024)}, f32[1058]{0:T(1024)S(1)}, u32[]{:S(2)}) copy-start(f32[1058]{0:T(1024)S(1)} %broadcast_multiply_fusion.1) | copy-start | bytes 12700
  8.2 93.8 %copy-start.26 = (f32[1058]{0:T(1024)}, f32[1058]{0:T(1024)S(1)}, u32[]{:S(2)}) copy-start(f32[1058]{0:T(1024)S(1)} %fusion.30) | copy-start | bytes 12700
  8.3 104.1 %copy-start.20 = (f32[1058]{0:T(1024)}, f32[1058]{0:T(1024)S(1)}, u32[]{:S(2)}) copy-start(f32[1058]{0:T(1024)S(1)} %fusion.43) | copy-start | bytes 12700
  105.5 6.9 %copy-start.34 = (f32[768]{0:T(1024)}, f32[768]{0:T(1024)S(1)}, u32[]{:S(2)}) copy-start(f32[768]{0:T(1024)S(1)} %reshape.378) | copy-start | bytes 9220
  105.7 6.7 %copy-start.36 = (f32[768]{0:T(1024)}, f32[768]{0:T(1024)S(1)}, u32[]{:S(2)}) copy-start(f32[768]{0:T(1024)S(1)} %reshape.379) | copy-start | bytes 9220
  196.3 7.7 %copy-start = (bf16[2,529,768]{1,2,0:T(8,128)(2,1)}, bf16[2,529,768]{1,2,0:T(8,128)(2,1)S(1)}, u32[]{:S(2)}) copy-start(bf16[2,529,768]{1,2,0:T(8,128)(2,1)S(1)} %get-tuple-element.423) | copy-start | bytes 4875268
  196.3 7.7 %copy-start.13 = (f32[2,12,529,1]{2,1,3,0:T(8,128)}, f32[2,12,529,1]{2,1,3,0:T(8,128)S(1)}, u32[]{:S(2)}) copy-start(f32[2,12,529,1]{2,1,3,0:T(8,128)S(1)} %get-tuple-element.371) | copy-start | bytes 152356
  196.3 7.7 %copy-start.15 = (pred[2,529]{1,0:T(4,128)(4,1)}, pred[2,529]{1,0:T(4,128)(4,1)S(1)}, u32[]{:S(2)}) copy-start(pred[2,529]{1,0:T(4,128)(4,1)S(1)} %get-tuple-element.426) | copy-start | bytes 3178
  196.3 9.3 %slice-start = ((s8[4718592]{0:T(1024)(128)(4,1)}), s8[524288]{0:T(1024)(128)(4,1)S(1)}, s32[]{:S(2)}) async-start(s8[4718592]{0:T(1024)(128)(4,1)} %bitcast.172), calls=%async_computation | async-start | bytes 1048576
  200.0 5.6 %slice-start.1 = ((s8[4718592]{0:T(1024)(128)(4,1)}), s8[4194304]{0:T(1024)(128)(4,1)S(1)}, s32[]{:S(2)}) async-start(s8[4718592]{0:T(1024)(128)(4,1)} %bitcast.172), calls=%async_computation.1 | async-start | bytes 8388608
  204.0 37.3 %copy-start.6 = (f32[1058,768]{1,0:T(8,128)}, f32[1058,768]{1,0:T(8,128)S(1)}, u32[]{:S(2)}) copy-start(f32[1058,768]{1,0:T(8,128)S(1)} %get-tuple-element.224) | copy-start | bytes 9750532
  204.6 1.0 copy-start.28
  205.6 35.8 %copy-start.24 = (f32[1058]{0:T(1024)S(1)}, f32[1058]{0:T(1024)}, u32[]{:S(2)}) copy-start(f32[1058]{0:T(1024)} %reshape.387) | copy-start | bytes 12700
  241.3 17.3 %copy-start.7 = (f32[1058,768]{1,0:T(8,128)S(1)}, f32[1058,768]{1,0:T(8,128)}, u32[]{:S(2)}) copy-start(f32[1058,768]{1,0:T(8,128)} %copy-done.6) | copy-start | bytes 9750532
  241.3 17.3 %copy-start.38 = (f32[768]{0:T(1024)S(1)}, f32[768]{0:T(1024)}, u32[]{:S(2)}) copy-start(f32[768]{0:T(1024)} %reshape.386) | copy-start | bytes 9220
  258.6 10.3 %copy-start.9 = (bf16[1058,768]{1,0:T(8,128)(2,1)S(1)}, bf16[1058,768]{1,0:T(8,128)(2,1)}, u32[]{:S(2)}) copy-start(bf16[1058,768]{1,0:T(8,128)(2,1)} %param.22) | copy-start | bytes 4875268
  258.6 10.3 %copy-start.41 = (bf16[1058,3072]{1,0:T(8,128)(2,1)S(1)}, bf16[1058,3072]{1,0:T(8,128)(2,1)}, u32[]{:S(2)}) copy-start(bf16[1058,3072]{1,0:T(8,128)(2,1)} %get-tuple-element.200) | copy-start | bytes 19501060
  268.9 9.1 %copy-start.39 = (bf16[2,2,4,2,24,3072]{5,4,3,2,1,0:T(8,128)(2,1)S(1)}, bf16[2,2,4,2,24,3072]{5,4,3,2,1,0:T(8,128)(2,1)}, u32[]{:S(2)}) copy-start(bf16[2,2,4,2,24,3072]{5,4,3,2,1,0:T(8,128)(2,1)} %get-tuple-element.109) | copy-start | bytes 14155780
  268.9 9.1 %copy-start.40 = (bf16[1058,3072]{1,0:T(8,128)(2,1)S(1)}, bf16[1058,3072]{1,0:T(8,128)(2,1)}, u32[]{:S(2)}) copy-start(bf16[1058,3072]{1,0:T(8,128)(2,1)} %get-tuple-element.229) | copy-start | bytes 19501060
  278.0 6.0 %copy-start.29 = (f32[1058]{0:T(1024)S(1)}, f32[1058]{0:T(1024)}, u32[]{:S(2)}) copy-start(f32[1058]{0:T(1024)} %copy-done.28) | copy-start | bytes 12700
  278.0 6.0 %copy-start.8 = (f32[1058,768]{1,0:T(8,128)S(1)}, f32[1058,768]{1,0:T(8,128)}, u32[]{:S(2)}) copy-start(f32[1058,768]{1,0:T(8,128)} %copy-done.6) | copy-start | bytes 9750532
  285.2 10.9 %copy-start.1 = (f32[1058,768]{1,0:T(8,128)}, f32[1058,768]{1,0:T(8,128)S(1)}, u32[]{:S(2)}) copy-start(f32[1058,768]{1,0:T(8,128)S(1)} %get-tuple-element.199) | copy-start | bytes 9750532
  294.0 4.5 copy-start.22
  296.1 2.3 copy-start.11
  298.5 1.8 copy-start.12
  304.9 1.5 copy-start.14
  304.9 1.5 copy-start.16
  420.8 5.7 %copy-start.4 = (bf16[1058,768]{1,0:T(8,128)(2,1)S(1)}, bf16[1058,768]{1,0:T(8,128)(2,1)}, u32[]{:S(2)}) copy-start(bf16[1058,768]{1,0:T(8,128)(2,1)} %param.21) | copy-start | bytes 4875268
  420.8 5.7 %copy-start.19 = (f32[1058]{0:T(1024)S(1)}, f32[1058]{0:T(1024)}, u32[]{:S(2)}) copy-start(f32[1058]{0:T(1024)} %copy-done.18) | copy-start | bytes 12700
  420.8 5.7 %copy-start.35 = (f32[768]{0:T(1024)S(1)}, f32[768]{0:T(1024)}, u32[]{:S(2)}) copy-start(f32[768]{0:T(1024)} %copy-done.34) | copy-start | bytes 9220
  426.5 9.5 %copy-start.27 = (f32[1058]{0:T(1024)S(1)}, f32[1058]{0:T(1024)}, u32[]{:S(2)}) copy-start(f32[1058]{0:T(1024)} %copy-done.26) | copy-start | bytes 12700
  426.5 9.5 %copy-start.5 = (bf16[1058,2304]{1,0:T(8,128)(2,1)S(1)}, bf16[1058,2304]{1,0:T(8,128)(2,1)}, u32[]{:S(2)}) copy-start(bf16[1058,2304]{1,0:T(8,128)(2,1)} %reshape.371) | copy-start | bytes 14625796
  436.1 0.7 copy-start.21
  436.1 0.7 copy-start.37
  443.6 3.8 copy-start.23
  443.6 3.8 copy-start.25
  443.8 3.6 copy-start.2
  443.8 3.6 copy-start.10
  447.4 4.4 copy-start.33
  447.4 4.4 copy-start.31
  447.4 4.4 copy-start.30
  447.4 4.4 copy-start.32
  447.5 4.4 copy-start.17

commit v2 on v1

--- a/solution.py
+++ b/solution.py
@@ -1,3 +1,4 @@
+import functools
 from functools import partial
 
 import jax
@@ -350,6 +351,387 @@
         name="scatter_grads",
     )(*partials)
 
+
+STEP = 544
+KEYS = 640
+NEGATIVE = -1e30
+F32 = jnp.float32
+LOW = jnp.bfloat16
+VMEM = pltpu.VMEM
+
+
+def dot(a, b):
+    return lax.dot_general(a, b, (((1,), (0,)), ((), ())), preferred_element_type=F32)
+
+
+def dot_t(a, b):
+    return lax.dot_general(a, b, (((1,), (1,)), ((), ())), preferred_element_type=F32)
+
+
+def lanes_of(shape):
+    return lax.broadcasted_iota(jnp.int32, shape, 1)
+
+
+def standard(rows):
+    width = rows.shape[-1]
+    centred = rows - jnp.sum(rows, axis=-1, keepdims=True) * (1.0 / width)
+    spread = jnp.sum(centred * centred, axis=-1, keepdims=True) * (1.0 / width)
+    inverse = lax.rsqrt(spread + epsilon)
+    return centred * inverse, inverse
+
+
+def standard_back(normed, inverse, e):
+    width = e.shape[-1]
+    mean_e = jnp.sum(e, axis=-1, keepdims=True) * (1.0 / width)
+    mean_en = jnp.sum(e * normed, axis=-1, keepdims=True) * (1.0 / width)
+    return (e - mean_e - normed * mean_en) * inverse
+
+
+def first_norm(x_ref, vec_ref, hn_ref, hnt_ref):
+    tokens = x_ref.shape[0]
+    tile = 128
+
+    def one(i, carry):
+        rows = pl.ds(pl.multiple_of(i * tile, tile), tile)
+        n, _ = standard(x_ref[rows, :].astype(F32))
+        hn = (n * vec_ref[0:1, :] + vec_ref[1:2, :]).astype(LOW)
+        hn_ref[rows, :] = hn
+        hnt_ref[:, rows] = hn.T
+        return carry
+
+    whole = tokens // tile
+    lax.fori_loop(0, whole, one, 0)
+    rest = tokens - whole * tile
+    n, _ = standard(x_ref[whole * tile :, :].astype(F32))
+    hn = (n * vec_ref[0:1, :] + vec_ref[1:2, :]).astype(LOW)
+    hn_ref[whole * tile :, :] = hn
+    padded = jnp.concatenate([hn, jnp.zeros((tile - rest, hn.shape[1]), LOW)], axis=0)
+    hnt_ref[:, whole * tile :] = padded.T
+
+
+def project_qkv(hn_ref, w_ref, bias_ref, qkv_ref):
+    tokens, columns = hn_ref.shape[0], 256
+    n = w_ref.shape[1] // columns
+    qkv_ref[tokens:, :] = jnp.zeros((qkv_ref.shape[0] - tokens, qkv_ref.shape[1]), LOW)
+
+    def one(j, carry):
+        cols = pl.ds(pl.multiple_of(j * columns, columns), columns)
+        bias = bias_ref[0:1, cols]
+        weight = w_ref[:, cols]
+        for b in range(tokens // STEP):
+            rows = slice(b * STEP, (b + 1) * STEP)
+            qkv_ref[rows, cols] = (dot(hn_ref[rows, :], weight) + bias).astype(LOW)
+        return carry
+
+    lax.fori_loop(0, n, one, 0)
+
+
+def attend(b, pair, qkv_ref, augk_ref, o_ref, augq_ref, width):
+    base = pl.multiple_of(b * STEP, STEP)
+    lane = pl.multiple_of(pair * 128, 128)
+    q = qkv_ref[pl.ds(base, STEP), pl.ds(lane, 128)]
+    k = qkv_ref[pl.ds(base, KEYS), pl.ds(width + lane, 128)]
+    v = qkv_ref[pl.ds(base, KEYS), pl.ds(2 * width + lane, 128)]
+    augk = augk_ref[b]
+    half_q = lanes_of(q.shape) < 64
+    half_k = lanes_of(k.shape) < 64
+    start = jnp.where(lanes_of(q.shape) % 64 == 0, 1.0, 0.0).astype(LOW)
+    ones = jnp.ones(v.shape, LOW)
+    peaks, outs = [], []
+    for h in range(2):
+        side_q = half_q if h == 0 else ~half_q
+        side_k = half_k if h == 0 else ~half_k
+        raw = dot_t(jnp.where(side_q, q, start), jnp.where(side_k, k, augk))
+        peak = jnp.max(raw, axis=-1, keepdims=True)
+        p = jnp.exp((raw - peak) * 0.125).astype(LOW)
+        outs.append(dot(p, jnp.where(side_k, v, ones)))
+        peaks.append(peak)
+    half = lanes_of(outs[0].shape) < 64
+    data = jnp.where(half, outs[0], outs[1])
+    total_other = jnp.where(half, outs[1], outs[0])
+    total = pltpu.roll(total_other, 64, 1)
+    o_ref[pl.ds(base, STEP), pl.ds(lane, 128)] = (data / total).astype(LOW)
+    level = jnp.where(half, peaks[1], peaks[0]) + 8.0 * jnp.log(total_other)
+    high = level.astype(LOW)
+    rest = level - high.astype(F32)
+    mid = rest.astype(LOW)
+    last = (rest - mid.astype(F32)).astype(LOW)
+    spot = lanes_of(high.shape) % 64
+    zero = jnp.zeros_like(high)
+    aug = jnp.where(spot == 0, jnp.ones_like(high),
+          jnp.where(spot == 1, -high, jnp.where(spot == 2, -mid, jnp.where(spot == 3, -last, zero))))
+    slot = b * (width // 128) + pair
+    augq_ref[slot, 0:STEP, :] = aug
+    tail = (KEYS - STEP, 128)
+    augq_ref[slot, STEP:KEYS, :] = jnp.where(lanes_of(tail) % 64 == 1, NEGATIVE, 0.0).astype(LOW)
+
+
+def attend_back(b, pair, qkv_ref, augk_ref, augq_ref, do_ref, o_ref, dqkv_ref, width):
+    base = pl.multiple_of(b * STEP, STEP)
+    lane = pl.multiple_of(pair * 128, 128)
+    wide, rows, cols = pl.ds(base, KEYS), pl.ds(base, STEP), pl.ds(lane, 128)
+    q = qkv_ref[wide, cols]
+    k = qkv_ref[rows, pl.ds(width + lane, 128)]
+    v = qkv_ref[rows, pl.ds(2 * width + lane, 128)]
+    do = do_ref[wide, cols]
+    augq = augq_ref[b * (width // 128) + pair]
+    augk = augk_ref[b, 0:STEP, :]
+    shape_q, shape_k = (KEYS, 128), (STEP, 128)
+    prod = do.astype(F32) * o_ref[wide, cols].astype(F32)
+    high = prod.astype(LOW)
+    mid = (prod - high.astype(F32)).astype(LOW)
+    swap = ((lax.broadcasted_iota(jnp.int32, (128, 128), 0) < 64) != (lanes_of((128, 128)) < 64)).astype(F32).astype(LOW)
+    delta = dot(high, swap) + dot(mid, swap)
+    high = delta.astype(LOW)
+    mid = (delta - high.astype(F32)).astype(LOW)
+    spot = lanes_of(shape_q) % 64
+    augdo = jnp.where(spot == 0, -high, jnp.where(spot == 1, -mid, jnp.zeros_like(high)))
+    augv = jnp.where(lanes_of(shape_k) % 64 < 2, 1.0, 0.0).astype(LOW)
+    half_q, half_k = lanes_of(shape_q) < 64, lanes_of(shape_k) < 64
+    kt = k.T
+    dks, dvs, dqs = [], [], []
+    for h in range(2):
+        side_q = half_q if h == 0 else ~half_q
+        side_k = half_k if h == 0 else ~half_k
+        raw = dot_t(jnp.where(side_k, k, augk), jnp.where(side_q, q, augq))
+        p = jnp.exp(raw * 0.125)
+        dp = dot_t(jnp.where(side_k, v, augv), jnp.where(side_q, do, augdo))
+        ds = (p * dp).astype(LOW)
+        dvs.append(dot(p.astype(LOW), do))
+        dks.append(dot(ds, q))
+        dqs.append(dot(kt, ds))
+    dqt = jnp.concatenate([dqs[0][:64], dqs[1][64:]], axis=0) * 0.125
+    dqkv_ref[rows, cols] = dqt.T[0:STEP, :].astype(LOW)
+    dqkv_ref[rows, pl.ds(width + lane, 128)] = (jnp.where(half_k, dks[0], dks[1]) * 0.125).astype(LOW)
+    dqkv_ref[rows, pl.ds(2 * width + lane, 128)] = jnp.where(half_k, dvs[0], dvs[1]).astype(LOW)
+
+
+def project_out(o_ref, w_ref, x_ref, vec_ref, r_ref, ot_ref):
+    tokens = x_ref.shape[0]
+    for b in range(tokens // STEP):
+        rows = slice(b * STEP, (b + 1) * STEP)
+        r_ref[rows, :] = x_ref[rows, :].astype(F32) + (dot(o_ref[rows, :], w_ref[...]) + vec_ref[4:5, :])
+    tile = 128
+
+    def one(i, carry):
+        rows = pl.ds(pl.multiple_of(i * tile, tile), tile)
+        ot_ref[:, rows] = o_ref[rows, :].T
+        return carry
+
+    lax.fori_loop(0, ot_ref.shape[1] // tile, one, 0)
+
+
+def forward_body(x_ref, vec_ref, bias_ref, wq_ref, wp_ref, augk_ref, qkv_ref, o_ref, augq_ref, r_ref, hnt_ref, ot_ref, hn_ref):
+    width = x_ref.shape[1]
+    tokens = x_ref.shape[0]
+    first_norm(x_ref, vec_ref, hn_ref, hnt_ref)
+    project_qkv(hn_ref, wq_ref, bias_ref, qkv_ref)
+    o_ref[tokens:, :] = jnp.zeros((o_ref.shape[0] - tokens, width), LOW)
+    pairs = width // 128
+
+    def one(i, carry):
+        attend(i // pairs, i % pairs, qkv_ref, augk_ref, o_ref, augq_ref, width)
+        return carry
+
+    lax.fori_loop(0, pairs * (tokens // STEP), one, 0)
+    project_out(o_ref, wp_ref, x_ref, vec_ref, r_ref, ot_ref)
+
+
+def sizes(tokens):
+    tall = tokens + KEYS - STEP
+    even = -(-tokens // 128) * 128
+    return tall, even
+
+
+def forward_attention(x, vec, bias, wq, wp, augk):
+    tokens, width = x.shape
+    tall, even = sizes(tokens)
+    items = tokens // STEP
+    out = [((tall, 3 * width), LOW), ((tall, width), LOW), ((items * (width // 128), KEYS, 128), LOW),
+           ((tokens, width), F32), ((width, even), LOW), ((width, even), LOW)]
+    return pl.pallas_call(
+        forward_body,
+        out_shape=[jax.ShapeDtypeStruct(s, d) for s, d in out],
+        in_specs=[pl.BlockSpec(memory_space=VMEM)] * 6,
+        out_specs=[pl.BlockSpec(memory_space=VMEM)] * 6,
+        scratch_shapes=[pltpu.VMEM((tokens, width), LOW)],
+        compiler_params=pltpu.CompilerParams(vmem_limit_bytes=58 << 20),
+        name="forward_attention",
+    )(x, vec, bias, wq, wp, augk)
+
+
+ERFC = (-0.028961464762687683, 0.13991104066371918, -0.23952563107013702, 0.13530659675598145, -0.011358031071722507, 0.10075884312391281, 0.12164358794689178, 0.14118188619613647, 0.14104320108890533)
+
+
+def gelu_parts(u):
+    t = pl.reciprocal(1.0 + (0.5 * 0.5 ** 0.5) * jnp.abs(u), approx=False)
+    poly = jnp.full_like(t, ERFC[0])
+    for c in ERFC[1:]:
+        poly = poly * t + c
+    bell = jnp.exp(-0.5 * (u * u))
+    tail = poly * t * bell
+    phi = jnp.where(u >= 0, 1.0 - tail, tail)
+    return u * phi, phi + u * (bell * 0.3989422804014327)
+
+
+def mlp_body(chunk, r_ref, dy_ref, vec_ref, up_bias_ref, wu_ref, wd_ref,
+             out_ref, dr_ref, sums_ref, gub_ref, gwu_ref, gwd_ref,
+             hm_ref, hmt_ref, m_ref, dhm_ref, du_ref):
+    step = pl.program_id(0)
+    steps = pl.num_programs(0)
+    tokens, width = r_ref.shape
+    even = hmt_ref.shape[1]
+    tile = 128
+    whole = tokens // tile
+
+    @pl.when(step == 0)
+    def _():
+        def one(i, carry):
+            rows = pl.ds(pl.multiple_of(i * tile, tile), tile)
+            n, _ = standard(r_ref[rows, :])
+            hm = (n * vec_ref[5:6, :] + vec_ref[6:7, :]).astype(LOW)
+            hm_ref[rows, :] = hm
+            hmt_ref[:, rows] = hm.T
+            return carry
+
+        lax.fori_loop(0, whole, one, 0)
+        n, _ = standard(r_ref[whole * tile :, :])
+        hm = (n * vec_ref[5:6, :] + vec_ref[6:7, :]).astype(LOW)
+        hm_ref[whole * tile :, :] = hm
+        rest = jnp.zeros((even - tokens, width), LOW)
+        hmt_ref[:, whole * tile :] = jnp.concatenate([hm, rest], axis=0).T
+        du_ref[tokens:, :] = jnp.zeros((even - tokens, chunk), LOW)
+        m_ref[...] = jnp.zeros_like(m_ref)
+        dhm_ref[...] = jnp.zeros_like(dhm_ref)
+
+    bias = up_bias_ref[0:1, :]
+    for b in range(tokens // STEP):
+        rows = slice(b * STEP, (b + 1) * STEP)
+        u = dot(hm_ref[rows, :], wu_ref[...]) + bias
+        gl, slope = gelu_parts(u)
+        gl = gl.astype(LOW)
+        dm = dy_ref[rows, :]
+        du = (dot_t(dm, wd_ref[...]) * slope).astype(LOW)
+        du_ref[rows, :] = du
+        m_ref[rows, :] += dot(gl, wd_ref[...])
+        dhm_ref[rows, :] += dot_t(du, wu_ref[...])
+        total = jnp.sum(du.astype(F32), axis=0, keepdims=True)
+        part = lax.dot_general(gl, dm, (((0,), (0,)), ((), ())), preferred_element_type=F32)
+        if b == 0:
+            ub_sum, down = total, part
+        else:
+            ub_sum, down = ub_sum + total, down + part
+    gub_ref[...] = jnp.broadcast_to(ub_sum, gub_ref.shape)
+    gwd_ref[...] = down.astype(LOW)
+    gwu_ref[...] = dot(hmt_ref[...], du_ref[...]).astype(LOW)
+
+    @pl.when(step == steps - 1)
+    def _():
+        sums_ref[...] = jnp.zeros_like(sums_ref)
+
+        def back(rows):
+            r = r_ref[rows, :]
+            n, inverse = standard(r)
+            dy = dy_ref[rows, :].astype(F32)
+            dhm = dhm_ref[rows, :]
+            out_ref[rows, :] = (r + (m_ref[rows, :] + vec_ref[7:8, :])).astype(LOW)
+            dr_ref[rows, :] = dy + standard_back(n, inverse, dhm * vec_ref[5:6, :])
+            sums_ref[0:1, :] += jnp.sum(dhm * n, axis=0, keepdims=True)
+            sums_ref[1:2, :] += jnp.sum(dhm, axis=0, keepdims=True)
+            sums_ref[2:3, :] += jnp.sum(dy, axis=0, keepdims=True)
+
+        def one(i, carry):
+            back(pl.ds(pl.multiple_of(i * 64, 64), 64))
+            return carry
+
+        lax.fori_loop(0, tokens // 64, one, 0)
+
+
+def feed_forward(r, dy, vec, up_bias, wu, wd, chunk=512):
+    tokens, width = r.shape
+    hidden = wu.shape[1]
+    _, even = sizes(tokens)
+    whole = lambda *s: pl.BlockSpec(s, lambda j: (0,) * len(s))
+    return pl.pallas_call(
+        functools.partial(mlp_body, chunk),
+        grid=(hidden // chunk,),
+        out_shape=[jax.ShapeDtypeStruct((tokens, width), LOW), jax.ShapeDtypeStruct((tokens, width), F32),
+                   jax.ShapeDtypeStruct((8, width), F32), jax.ShapeDtypeStruct((8, hidden), F32),
+                   jax.ShapeDtypeStruct((width, hidden), LOW), jax.ShapeDtypeStruct((hidden, width), LOW)],
+        in_specs=[whole(tokens, width), whole(tokens, width), whole(8, width),
+                  pl.BlockSpec((8, chunk), lambda j: (0, j)),
+                  pl.BlockSpec((width, chunk), lambda j: (0, j)),
+                  pl.BlockSpec((chunk, width), lambda j: (j, 0))],
+        out_specs=[whole(tokens, width), whole(tokens, width), whole(8, width),
+                   pl.BlockSpec((8, chunk), lambda j: (0, j)),
+                   pl.BlockSpec((width, chunk), lambda j: (0, j)),
+                   pl.BlockSpec((chunk, width), lambda j: (j, 0))],
+        scratch_shapes=[pltpu.VMEM((tokens, width), LOW), pltpu.VMEM((width, even), LOW),
+                        pltpu.VMEM((tokens, width), F32), pltpu.VMEM((tokens, width), F32),
+                        pltpu.VMEM((even, chunk), LOW)],
+        compiler_params=pltpu.CompilerParams(vmem_limit_bytes=58 << 20),
+        name="feed_forward",
+    )(r, dy, vec, up_bias, wu, wd)
+
+
+def backward_body(x_ref, vec_ref, wq_ref, wp_ref, augk_ref, qkv_ref, o_ref, augq_ref, hnt_ref, ot_ref, dr_ref,
+                  dx_ref, gwq_ref, gwp_ref, sums_ref, gqb_ref, do_ref, da_ref, dqkv_ref):
+    tokens, width = x_ref.shape
+    pairs = width // 128
+    items = tokens // STEP
+    even = hnt_ref.shape[1]
+    da_ref[tokens:, :] = jnp.zeros((even - tokens, width), LOW)
+    do_ref[tokens:, :] = jnp.zeros((do_ref.shape[0] - tokens, width), LOW)
+    dqkv_ref[tokens:, :] = jnp.zeros((even - tokens, 3 * width), LOW)
+    sums_ref[...] = jnp.zeros_like(sums_ref)
+    for b in range(items):
+        rows = slice(b * STEP, (b + 1) * STEP)
+        da = dr_ref[rows, :].astype(LOW)
+        da_ref[rows, :] = da
+        sums_ref[0:1, :] += jnp.sum(da.astype(F32), axis=0, keepdims=True)
+        do_ref[rows, :] = dot_t(da, wp_ref[...]).astype(LOW)
+    gwp_ref[...] = dot(ot_ref[...], da_ref[...]).astype(LOW)
+
+    def group(g, carry):
+        def one(i, carry):
+            attend_back(i // 2, g * 2 + i % 2, qkv_ref, augk_ref, augq_ref, do_ref, o_ref, dqkv_ref, width)
+            return carry
+
+        lax.fori_loop(0, 2 * items, one, 0)
+        for part in range(3):
+            cols = pl.ds(pl.multiple_of(part * width + g * 256, 256), 256)
+            d = dqkv_ref[:, cols]
+            gwq_ref[:, cols] = dot(hnt_ref[...], d).astype(LOW)
+            gqb_ref[:, cols] = jnp.broadcast_to(jnp.sum(d.astype(F32), axis=0, keepdims=True), (8, 256))
+        return carry
+
+    lax.fori_loop(0, pairs // 2, group, 0)
+    for b in range(items):
+        rows = slice(b * STEP, (b + 1) * STEP)
+        dhn = dot_t(dqkv_ref[rows, :], wq_ref[...])
+        n, inverse = standard(x_ref[rows, :].astype(F32))
+        dx = dr_ref[rows, :] + standard_back(n, inverse, dhn * vec_ref[0:1, :])
+        dx_ref[rows, :] = dx.astype(LOW)
+        sums_ref[1:2, :] += jnp.sum(dhn * n, axis=0, keepdims=True)
+        sums_ref[2:3, :] += jnp.sum(dhn, axis=0, keepdims=True)
+
+
+def backward_attention(x, vec, wq, wp, augk, qkv, o, augq, hnt, ot, dr):
+    tokens, width = x.shape
+    tall, even = sizes(tokens)
+    return pl.pallas_call(
+        backward_body,
+        out_shape=[jax.ShapeDtypeStruct((tokens, width), LOW), jax.ShapeDtypeStruct((width, 3 * width), LOW),
+                   jax.ShapeDtypeStruct((width, width), LOW), jax.ShapeDtypeStruct((8, width), F32),
+                   jax.ShapeDtypeStruct((8, 3 * width), F32)],
+        in_specs=[pl.BlockSpec(memory_space=VMEM)] * 11,
+        out_specs=[pl.BlockSpec(memory_space=VMEM)] * 5,
+        scratch_shapes=[pltpu.VMEM((tall, width), LOW), pltpu.VMEM((even, width), LOW), pltpu.VMEM((even, 3 * width), LOW)],
+        compiler_params=pltpu.CompilerParams(vmem_limit_bytes=60 << 20),
+        name="backward_attention",
+    )(x, vec, wq, wp, augk, qkv, o, augq, hnt, ot, dr)
+
+
 def pack_vectors(eight, wide):
     block = jnp.stack(eight, axis=-2)
     rows = wide.reshape(wide.shape[:-1] + (4, -1))
@@ -362,6 +744,11 @@
 def unpack_vectors(blocks, share):
     eight = tuple(blocks[:, k, :share].reshape(-1) for k in range(8))
     return eight, blocks[:, :4, share : 2 * share].reshape(-1)
+
+
+def pad_rows(rows, items, length, step):
+    parts = rows.reshape(items, length, -1)
+    return jnp.pad(parts, ((0, 0), (0, step - length), (0, 0))).reshape(items * step, -1)
 
 
 def local(
@@ -383,13 +770,18 @@
     w_down,
     down_bias,
 ):
-    items_here = counts.shape[0]
-    length = blank_mask.shape[1]
+    items, length = blank_mask.shape
     width = patches.shape[1]
+    share = w_qkv.shape[0]
     positions = jnp.arange(length, dtype=jnp.int32)
-    live_mask = positions[None, :] < counts[:, None]
-    allowed = live_mask & ((blank_mask == 1) | (positions[None, :] == 0))
-    live_rows = live_mask.reshape(-1, 1).astype(jnp.float32)
+    live = positions[None, :] < counts[:, None]
+    allowed = live & ((blank_mask == 1) | (positions[None, :] == 0))
+    bias = jnp.where(allowed, 0.0, NEGATIVE)
+    bias = jnp.pad(bias, ((0, 0), (0, KEYS - length)), constant_values=NEGATIVE)
+    spot = jnp.arange(128) % HEAD_DIM
+    augk = jnp.where(spot == 0, bias[:, :, None], jnp.where(spot < 4, 1.0, 0.0)).astype(LOW)
+    x = pad_rows(patches, items, length, STEP)
+    dy = pad_rows(jnp.where(live.reshape(-1, 1), cotangent, 0), items, length, STEP)
     vectors = pack_vectors(
         (ln1_gain, ln1_shift, query_bias, value_bias, proj_bias, ln2_gain, ln2_shift, down_bias),
         up_bias,
@@ -397,146 +789,64 @@
     all_qkv, all_vectors, all_proj, all_up, all_down = gather_all(
         (w_qkv, vectors, w_proj, w_up, w_down), (0, 0, 3, 4, 7)
     )
-    qkv_weight = all_qkv.reshape(width, -1)
-    proj_weight = all_proj.reshape(width, width)
-    up_weight = all_up.reshape(width, -1)
-    down_weight = all_down.reshape(-1, width)
-    (
-        gain_one,
-        shift_one,
-        bias_query,
-        bias_value,
-        bias_proj,
-        gain_two,
-        shift_two,
-        bias_down,
-    ), bias_up = unpack_vectors(all_vectors.reshape(-1, 8, 128), w_qkv.shape[0])
-    inputs = patches.astype(jnp.float32)
-    gain_float = gain_one.astype(jnp.float32)
-    shift_float = shift_one.astype(jnp.float32)
-    normed_low = normalize(inputs, gain_float, shift_float).astype(jnp.bfloat16)
-    projected = jnp.dot(normed_low, qkv_weight, preferred_element_type=jnp.float32)
-    queries = (projected[:, :width] + bias_query.astype(jnp.float32)).astype(jnp.bfloat16)
-    keys_all = projected[:, width : 2 * width].astype(jnp.bfloat16)
-    values_all = (projected[:, 2 * width :] + bias_value.astype(jnp.float32)).astype(jnp.bfloat16)
-    per_item = (
-        queries.reshape(items_here, length, width),
-        keys_all.reshape(items_here, length, width),
-        values_all.reshape(items_here, length, width),
-        allowed,
-    )
-    mixed_items, log_totals = lax.map(attend_forward, per_item)
-    mixed_low = mixed_items.reshape(-1, width)
-    residual = (
-        inputs
-        + jnp.dot(mixed_low, proj_weight, preferred_element_type=jnp.float32)
-        + bias_proj.astype(jnp.float32)
-    )
-    normed_two = normalize(
-        residual, gain_two.astype(jnp.float32), shift_two.astype(jnp.float32)
-    ).astype(jnp.bfloat16)
-    pre_act = jnp.dot(normed_two, up_weight, preferred_element_type=jnp.float32) + bias_up.astype(
-        jnp.float32
-    )
-    activated, gelu_back = jax.vjp(partial(jax.nn.gelu, approximate=False), pre_act)
-    act_low = activated.astype(jnp.bfloat16)
-    out_branch = jnp.dot(
-        act_low, down_weight, preferred_element_type=jnp.float32
-    ) + bias_down.astype(jnp.float32)
-    output = ((residual + out_branch) * live_rows).astype(jnp.bfloat16)
-    grad_out = cotangent.astype(jnp.float32) * live_rows
-    grad_down_low = grad_out.astype(jnp.bfloat16)
-    down_grad = jnp.einsum("tf,td->fd", act_low, grad_down_low, preferred_element_type=jnp.float32)
-    down_bias_grad = jnp.sum(grad_down_low.astype(jnp.float32), axis=0)
-    grad_act = jnp.einsum(
-        "td,fd->tf", grad_down_low, down_weight, preferred_element_type=jnp.float32
-    )
-    grad_pre_low = gelu_back(grad_act)[0].astype(jnp.bfloat16)
-    up_grad = jnp.einsum("td,tf->df", normed_two, grad_pre_low, preferred_element_type=jnp.float32)
-    up_bias_grad = jnp.sum(grad_pre_low.astype(jnp.float32), axis=0)
-    grad_normed_two = jnp.einsum(
-        "tf,df->td", grad_pre_low, up_weight, preferred_element_type=jnp.float32
-    )
-    _, norm_back_two = jax.vjp(
-        normalize, residual, gain_two.astype(jnp.float32), shift_two.astype(jnp.float32)
-    )
-    grad_resid_part, gain_two_grad, shift_two_grad = norm_back_two(grad_normed_two)
-    grad_resid = grad_out + grad_resid_part
-    grad_branch_low = grad_resid.astype(jnp.bfloat16)
-    proj_grad = jnp.einsum(
-        "td,te->de", mixed_low, grad_branch_low, preferred_element_type=jnp.float32
-    )
-    proj_bias_grad = jnp.sum(grad_branch_low.astype(jnp.float32), axis=0)
-    grad_mixed = jnp.einsum(
-        "te,de->td", grad_branch_low, proj_weight, preferred_element_type=jnp.float32
-    ).astype(jnp.bfloat16)
-    back_items = (
-        per_item[0],
-        per_item[1],
-        per_item[2],
-        allowed,
-        log_totals,
-        grad_mixed.reshape(items_here, length, width),
-    )
-    grad_projected = lax.map(attend_backward, back_items).reshape(-1, 3 * width)
-    qkv_grad = jnp.einsum(
-        "td,te->de", normed_low, grad_projected, preferred_element_type=jnp.float32
-    )
-    query_bias_grad = jnp.sum(grad_projected[:, :width].astype(jnp.float32), axis=0)
-    value_bias_grad = jnp.sum(grad_projected[:, 2 * width :].astype(jnp.float32), axis=0)
-    grad_normed = jnp.einsum(
-        "te,de->td", grad_projected, qkv_weight, preferred_element_type=jnp.float32
-    )
-    _, norm_back_one = jax.vjp(
-        normalize, inputs, gain_one.astype(jnp.float32), shift_one.astype(jnp.float32)
-    )
-    grad_input_part, gain_one_grad, shift_one_grad = norm_back_one(grad_normed)
-    grad_input = (grad_resid + grad_input_part).astype(jnp.bfloat16)
-    packed = pack_vectors(
-        tuple(
-            v.reshape(-1, w_qkv.shape[0])
-            for v in (
-                gain_one_grad,
-                shift_one_grad,
-                query_bias_grad,
-                value_bias_grad,
-                proj_bias_grad,
-                gain_two_grad,
-                shift_two_grad,
-                down_bias_grad,
-            )
-        ),
-        up_bias_grad.reshape(-1, up_bias.shape[0]),
-    )
-    low = jnp.bfloat16
+    wq = all_qkv.reshape(width, -1)
+    wp = all_proj.reshape(width, width)
+    wu = all_up.reshape(width, -1)
+    wd = all_down.reshape(-1, width)
+    eight, up = unpack_vectors(all_vectors.reshape(-1, 8, 128).astype(F32), share)
+    vec = jnp.stack(eight)
+    qkv_bias = jnp.broadcast_to(
+        jnp.concatenate([eight[2], jnp.zeros_like(eight[2]), eight[3]])[None], (8, 3 * width)
+    )
+    qkv, o, augq, r, hnt, ot = forward_attention(x, vec, qkv_bias, wq, wp, augk)
+    out, dr, sums_mlp, gub, gwu, gwd = feed_forward(
+        r, dy, vec, jnp.broadcast_to(up[None], (8, up.shape[0])), wu, wd
+    )
+    dx, gwq, gwp, sums_attn, gqb = backward_attention(x, vec, wq, wp, augk, qkv, o, augq, hnt, ot, dr)
+    gains = (
+        sums_attn[1],
+        sums_attn[2],
+        gqb[0, :width],
+        gqb[0, 2 * width :],
+        sums_attn[0],
+        sums_mlp[0],
+        sums_mlp[1],
+        sums_mlp[2],
+    )
+    packed = pack_vectors(tuple(v.reshape(-1, share) for v in gains), gub[0].reshape(-1, 4 * share))
     blocks = tuple(
         t.reshape((2, 2, 4, 2) + s)
         for t, s in (
-            (down_grad.astype(low), w_down.shape),
-            (up_grad.astype(low), w_up.shape),
-            (proj_grad.astype(low), w_proj.shape),
-            (qkv_grad.astype(low), w_qkv.shape),
+            (gwd, w_down.shape),
+            (gwu, w_up.shape),
+            (gwp, w_proj.shape),
+            (gwq, w_qkv.shape),
             (packed, (8, 128)),
         )
     )
     own_down, own_up, own_proj, own_qkv, own_packed = scatter_all(blocks, (0, 3, 6, 7, 8))
-    own_vectors, own_up_bias = unpack_vectors(own_packed[None], w_qkv.shape[0])
+    own, own_up_bias = unpack_vectors(own_packed[None], share)
+
+    def unpad(rows):
+        return rows.reshape(items, STEP, width)[:, :length].reshape(items * length, width)
+
+    output = jnp.where(live.reshape(-1, 1), unpad(out), 0)
     return (
         output,
-        grad_input,
-        own_vectors[0],
-        own_vectors[1],
+        unpad(dx),
+        own[0],
+        own[1],
         own_qkv,
-        own_vectors[2],
-        own_vectors[3],
+        own[2],
+        own[3],
         own_proj,
-        own_vectors[4],
-        own_vectors[5],
-        own_vectors[6],
+        own[4],
+        own[5],
+        own[6],
         own_up,
         own_up_bias,
         own_down,
-        own_vectors[7],
+        own[7],
     )
 
 

time: 555 us -> 360 us (0.65); the launches traced: 546 us -> 359 us
  matrix products: 218 us -> 0 us
  Pallas kernels: 182 us -> 332 us
  other arithmetic: 65.7 us -> 6.51 us
  local copies, waits for them, and re-layouts: 77.6 us -> 19.8 us
    dot_general x26 -> x0, matrix products: 218 us -> none  [the longest x1 35.7 us: local(): jnp.dot(normed_two, up_weight, preferred_element_type=jnp.float32)]
    pallas_call x0 -> x3, Pallas kernels: none -> 149 us  [the longest x1 61.1 us: feed_forward(): pl.pallas_call(functools.partial(mlp_body, chunk), grid=(hidden // chunk,...]
    reduce_sum x9 -> x0, other arithmetic: 30.2 us -> none  [the longest x2 18.3 us: attend_forward(): jnp.sum(jnp.exp(masked - peak), axis=-1, keepdims=True)]
    convert_element_type x8 -> x2, other arithmetic: 31.5 us -> 1.81 us  [the longest x1 0.96 us: local(): jnp.where(spot == 0, bias[:, :, None], jnp.where(spot < 4, 1.0, 0.0))]
    dynamic_update_slice x8 -> x0, local copies, waits for them, and re-layouts: 20.5 us -> none  [the longest x4 15.6 us: local(): grad_projected = lax.map(attend_backward, back_items).reshape(-1, 3 * width)]
    dynamic_slice x16 -> x0, local copies, waits for them, and re-layouts: 15.2 us -> none  [local(): mixed_items, log_totals = lax.map(attend_forward, per_item)]
    reshape x6 -> x4, local copies, waits for them, and re-layouts: 16.8 us -> 2.45 us  [the longest x2 1.8 us: unpad(): rows.reshape(items, STEP, width)[:, :length].reshape(items * length, width)]
    while x3 -> x0, local copies, waits for them, and re-layouts: 10.6 us -> none  [local(): mixed_items, log_totals = lax.map(attend_forward, per_item)]
where the time goes in v2:
time: 360 us; the launch traced here: 359 us
  Pallas kernels  332 us (92%)
  local copies, waits for them, and re-layouts  19.8 us (6%)
  other arithmetic  6.51 us (2%)
    pallas_call x1, Pallas kernels, gather_all(): pl.pallas_call(body, out_shape=[jax.ShapeDtypeStruct((2, 2, 4, 2) + s.sha...  92.7 us
    pallas_call x1, Pallas kernels, scatter_all(): pl.pallas_call(body, out_shape=[jax.ShapeDtypeStruct(p.shape[4:], jnp.flo...  90.4 us
    pallas_call x1, Pallas kernels, feed_forward(): pl.pallas_call(functools.partial(mlp_body, chunk), grid=(hidden // chunk,...  61.1 us
    pallas_call x1, Pallas kernels, backward_attention(): pl.pallas_call(backward_body, out_shape=[jax.ShapeDtypeStruct((tokens, wi...  48.7 us
    pallas_call x1, Pallas kernels, forward_attention(): pl.pallas_call(forward_body, out_shape=[jax.ShapeDtypeStruct(s, d) for s,...  39 us

profile of v2, /device:TPU:0, one launch (start us, length us, event | category | flops | bytes accessed | tf_op | source)
XLA Modules:
  0.0 359.2 jit_solution(10686823951126159564)
XLA Ops:
  0.7 0.7 reshape.117
  1.4 0.8 and_select_fusion
  2.2 0.8 stack.41
  3.1 0.6 pad.29.refs_1_
  3.7 0.7 iota_compare_fusion.1
  4.4 0.1 lt.37
  4.5 1.0 select_convert_fusion.augk_ref
  5.4 1.6 broadcast_select_fusion.1
  7.1 0.3 reshape.120
  7.4 1.3 pad.31
  8.7 0.7 copy-done.1
  9.5 0.3 reshape.115
  9.8 1.3 pad.27
  11.1 92.7 %gather_weights.1 = (bf16[2,2,4,2,24,2304]{5,4,3,2,1,0:T(8,128)(2,1)}, bf16[2,2,4,2,8,128]{5,4,3,2,1,0:T(8,128)(2,1)}, bf16[2,2,4,2,24,768]{5,4,3,2,1,0:T(8,128)...) custom-call(bf16[24,2304]{1,0:T(8,128)(2,1)} %refs_0_.1, bf16[8,128]{1,0:T(8,128)(2,1)} %pad.29.refs_1_, ...), custom_call_target="tpu_custom_call" | custom-call | tf_op jit(solution)/shard_map/gather_weights/pallas_call | solution.py:222
  103.8 0.9 bitcast_convert_fusion
  104.6 0.1 slice.124
  104.7 0.1 broadcast_in_dim.82
  104.9 0.4 fusion.2
  105.5 0.1 stack_reshape_squeeze.49
  105.6 0.1 stack_reshape_squeeze.52
  105.7 0.1 stack_reshape_squeeze.53
  105.9 0.1 stack_reshape_squeeze.51
  106.0 0.1 stack_reshape_squeeze.50
  106.1 0.1 stack_reshape_squeeze.55
  106.2 0.7 stack.42.vec_ref
  106.8 0.6 broadcast_in_dim.73.bias_ref
  107.4 0.6 broadcast_in_dim.83.up_bias_ref
  108.1 39.0 %forward_attention.1 = (bf16[1184,2304]{1,0:T(8,128)(2,1)}, bf16[1184,768]{1,0:T(8,128)(2,1)}, bf16[12,640,128]{2,1,0:T(8,128)(2,1)}, f32[1088,768]{1,0:T(8,128)...) custom-call(bf16[1088,768]{1,0:T(8,128)(2,1)} %bitcast.47, f32[8,768]{1,0:T(8,128)} %stack.42.vec_ref, ...), custom_call_target="tpu_custom_call" | custom-call | tf_op jit(solution)/shard_map/forward_attention/pallas_call | solution.py:552
  147.1 61.1 %feed_forward.1 = (bf16[1088,768]{1,0:T(8,128)(2,1)}, f32[1088,768]{1,0:T(8,128)}, f32[8,768]{1,0:T(8,128)}, f32[8,3072]{1,0:T(8,128)}, bf16[768,3072]{1,0:T(8,128)(2,1)}, /*index=5*/bf16[3072,768]{1,0:T(8,128)(2,1)}) custom-call(f32[1088,768]{1,0:T(8,128)} %get-tuple-element.45.r_ref, bf16[1088,768]{1,0:T(8,128)(2,1)} %bitcast.51, f32[8,768]{1,0:T(8,128)} %stack.42.vec_ref, ...), custom_call_target="tpu_custom_call" | custom-call | tf_op jit(solution)/shard_map/feed_forward/pallas_call | solution.py:655
  208.3 48.7 %backward_attention.1 = (bf16[1088,768]{1,0:T(8,128)(2,1)}, bf16[768,2304]{1,0:T(8,128)(2,1)}, bf16[768,768]{1,0:T(8,128)(2,1)}, f32[8,768]{1,0:T(8,128)}, f32[8,2304]{1,0:T(8,128)}) custom-call(bf16[1088,768]{1,0:T(8,128)(2,1)} %bitcast.48, f32[8,768]{1,0:T(8,128)} %stack.42.vec_ref, bf16[768,2304]{1,0:T(8,128)(2,1)} %bitcast.50, ...), custom_call_target="tpu_custom_call" | custom-call | tf_op jit(solution)/shard_map/backward_attention/pallas_call | solution.py:722
  256.9 0.1 slice.125
  257.1 0.3 reshape.125
  257.4 1.4 broadcast_select_fusion
  258.8 0.6 copy-done.3
  259.4 0.1 slice.126
  259.5 1.5 reshape.127
  261.0 0.9 slice_reduce_fusion.6
  261.9 0.9 slice_reduce_fusion.7
  263.1 0.9 slice_reduce_fusion.10
  264.4 0.1 reshape_reshape_squeeze.3
  264.6 0.1 select_maximum_fusion
  264.9 90.4 %scatter_grads.1 = (f32[96,768]{1,0:T(8,128)S(1)}, f32[24,3072]{1,0:T(8,128)S(1)}, f32[24,768]{1,0:T(8,128)S(1)}, f32[24,2304]{1,0:T(8,128)S(1)}, f32[8,128]{1,0:T(8,128)S(1)}) custom-call(bf16[2,2,4,2,96,768]{5,4,3,2,1,0:T(8,128)(2,1)} %bitcast.53, bf16[2,2,4,2,24,3072]{5,4,3,2,1,0:T(8,128)(2,1)} %bitcast.52, bf16[2,2,4,2,24,768]{5,4,3,2,1,0:T(8,128)(2,1)S(1)} %bitcast.43, ...), custom_call_target="tpu_custom_call" | custom-call | tf_op jit(solution)/shard_map/scatter_grads/pallas_call | solution.py:344
  355.3 0.6 reshape.133
  355.9 0.5 slice_bitcast_fusion
  356.5 0.7 copy.62
  357.2 0.6 copy.63
  357.8 0.7 copy.64
  358.5 0.7 copy.65
  (37 shorter events, 1.3 us)
Async XLA Ops:
  7.4 2.0 copy-start.1
  208.3 48.7 %copy-start.2 = (bf16[1088,768]{1,0:T(8,128)(2,1)S(1)}, bf16[1088,768]{1,0:T(8,128)(2,1)}, u32[]{:S(2)}) copy-start(bf16[1088,768]{1,0:T(8,128)(2,1)} %get-tuple-element.48) | copy-start | bytes 5013508
  257.4 2.0 copy-start.3
  259.5 5.3 %copy-start = (bf16[768,768]{1,0:T(8,128)(2,1)S(1)}, bf16[768,768]{1,0:T(8,128)(2,1)}, u32[]{:S(2)}) copy-start(bf16[768,768]{1,0:T(8,128)(2,1)} %get-tuple-element.58) | copy-start | bytes 3538948
